TPU v7x, 128 devices: a whole 4x4x4 slice. The times are simulated.
128 devices in a mesh: wave: 16 (over x, y), lat: 8 (over z, core).
Axes of the slice: x: 4, y: 4, z: 4, core: 2. Of those that a mesh axis runs over, the one named last changes fastest.
Arguments:
- control: bfloat16 [320, 641, 8, 137], P('wave', None, 'lat'), may hold values from -6 to 6
- spread: float32 [4, 640, 137], replicated, may hold values from 0.3 to 3
- vertical: bfloat16 [4, 137, 137], replicated, may hold values from -0.5 to 0.5
- legendre: bfloat16 [320, 641, 512], P('wave'), may hold values from -0.0048828125 to 0.0048828125
- column_index: int32 [65536], P(('wave', 'lat')), may hold values from 0 to 10239
- column_owner: int32 [65536, 1], P(('wave', 'lat')), may hold values from 0 to 127; in each aligned block of 512 rows (0 to 511, 512 to 1023, ...) at most 8 rows name the same one
- jacobian: bfloat16 [128, 366, 548], P(('wave', 'lat')), may hold values from -0.25 to 0.25
- channel_bias: float32 [128, 366], P(('wave', 'lat')), may hold values from -5 to 5
Outputs:
- departures: bfloat16 [65536, 366], P(('wave', 'lat'))
- increments: bfloat16 [65536, 548], P(('wave', 'lat'))
Inputs may be any that keep to these rules, and one draw needn't show every extreme that they name: `column_owner`: in each aligned block of 512 rows no owner appears more than 8 times, and some owner appears exactly 8 times.
All inputs are finite; a program needn't handle non-finite values.
Results may differ from a plain program's by a relative error of at most 0.0072.
Values may be sent and summed in bfloat16 or wider, within the bound.
No kernel may reach another device: no remote copies, remote signals or barrier semaphores. Data moves between devices by JAX's collectives and lax.ppermute only.
A program may use at most 128 MiB of HBM per device.

v0:
```python
import functools
import math

import jax
import jax.numpy as jnp
from jax import lax
from jax.experimental import pallas as pl
from jax.experimental.pallas import tpu as pltpu
from jax.sharding import PartitionSpec as P

NLON = 2560
LANES = 128
SLOT_LANES = 32
F32 = jnp.float32
BF16 = jnp.bfloat16


def dot(a, b):
    return jnp.dot(a, b, preferred_element_type=F32)


def fourier_kernel(
    base_ref, ctrl_ref, spread_ref, vert_ref, leg_ref, out_ref, main_s, rem_s, remt_s, tile_s
):
    slots = ctrl_ref.shape[3]
    waves = slots - 1
    modes = ctrl_ref.shape[2]
    rows = leg_ref.shape[2]
    dests = out_ref.shape[0]
    wide = spread_ref.shape[1]
    per_dest = rows // dests
    lane = lax.broadcasted_iota(jnp.int32, (1, wide), 1)
    spread = spread_ref[...]
    second_scale = pltpu.roll(spread, 1, 1)
    pair0 = base_ref[0] + pl.program_id(0) * 4
    for i in range(4):
        pair = pair0 + i
        first_scale = pltpu.roll(spread, wide - pair, 1)
        in_first = lane < waves - pair
        scale = jnp.where(in_first, first_scale, second_scale)[:, :slots]
        scaled = (ctrl_ref[i, 0].astype(F32) * scale).astype(BF16)
        spec = dot(vert_ref[...], scaled).astype(BF16)
        keep = in_first[:, :slots]
        zero = jnp.zeros_like(spec)
        first = jnp.where(keep, spec, zero)
        second = jnp.where(keep, zero, spec)
        both = jnp.concatenate([first[:, 256:], second[:, 256:]], axis=0)
        sums = dot(both, leg_ref[i, 256:, :])
        half_rows = spec.shape[0]
        parts = (sums[:half_rows] + dot(first[:, :256], leg_ref[i, :256, :]), sums[half_rows:])
        for h in range(2):
            j = 2 * i + h
            main_s[pl.ds(j, rows, stride=8), :] = jnp.transpose(parts[h][:LANES])
            rem_s[16 * j : 16 * j + 16, :] = parts[h][LANES:]
    remt_s[...] = jnp.transpose(rem_s[...])
    rem_rows = [remt_s[pl.ds(r, dests, stride=per_dest), :] for r in range(per_dest)]
    tile_lane = lax.broadcasted_iota(jnp.int32, (1, LANES), 1) // SLOT_LANES
    for j in range(8):
        tile = jnp.zeros((dests, LANES), F32)
        for r in range(per_dest):
            moved = pltpu.roll(rem_rows[r], (SLOT_LANES * r - 16 * j) % LANES, 1)
            tile = jnp.where(tile_lane == r, moved, tile)
        tile_s[pl.ds(j, dests, stride=8), :] = tile
    main = main_s[...].reshape(dests, per_dest, 8, LANES)
    for r in range(per_dest):
        out_ref[:, :, r * LANES : (r + 1) * LANES] = main[:, r].astype(BF16)
    out_ref[:, :, per_dest * LANES :] = tile_s[...].reshape(dests, 8, LANES).astype(BF16)


def fourier_blocks(control, spread, vertical, legendre, pair_base, dests):
    pairs, slots, _, modes = control.shape
    rows = legendre.shape[2]
    ctrl = jnp.transpose(control, (0, 2, 3, 1))
    wide = -(-slots // LANES) * LANES
    spread_t = jnp.pad(jnp.transpose(spread), ((0, 0), (0, wide - spread.shape[0])))
    vert = jnp.pad(vertical, ((0, 144 - vertical.shape[0]), (0, 0)))
    lanes = (rows // dests + 1) * LANES
    return pl.pallas_call(
        fourier_kernel,
        out_shape=jax.ShapeDtypeStruct((dests, 2 * pairs, lanes), BF16),
        grid=(pairs // 4,),
        in_specs=[
            pl.BlockSpec(memory_space=pltpu.SMEM),
            pl.BlockSpec((4, 1, modes, slots), lambda g: (g, 0, 0, 0)),
            pl.BlockSpec((modes, wide), lambda g: (0, 0)),
            pl.BlockSpec((144, modes), lambda g: (0, 0)),
            pl.BlockSpec((4, slots, rows), lambda g: (g, 0, 0)),
        ],
        out_specs=pl.BlockSpec((dests, 8, lanes), lambda g: (0, g, 0)),
        scratch_shapes=[
            pltpu.VMEM((rows * 8, LANES), F32),
            pltpu.VMEM((LANES, rows), F32),
            pltpu.VMEM((rows, LANES), F32),
            pltpu.VMEM((dests * 8, LANES), F32),
        ],
        name="fourier",
    )(pair_base, ctrl, spread_t, vert, legendre)


def cosine(turns):
    x = turns * math.pi
    y = x * x
    s = -1.0 / 39916800.0
    for c in (1.0 / 362880.0, -1.0 / 5040.0, 1.0 / 120.0, -1.0 / 6.0, 1.0):
        s = s * y + c
    s = s * x
    return 1.0 - 2.0 * (s * s)


def state_kernel(index_ref, owner_ref, coeff_ref, out_ref, spot_ref, table_s, row_s, state_s):
    v = pl.program_id(0)
    cols = table_s.shape[0]
    depth = table_s.shape[1]
    waves = depth // 2
    slots = out_ref.shape[0] // LANES
    sources = coeff_ref.shape[0]
    per_source = waves // sources

    @pl.when(v == 0)
    def _():
        column = jnp.transpose(jnp.broadcast_to(index_ref[...].astype(F32), (LANES, cols)))[:, :1]
        row = jnp.floor((column + 0.5) * (1.0 / NLON))
        longitude = column - row * NLON
        row_s[...] = jnp.broadcast_to(row, row_s.shape)
        lane = lax.broadcasted_iota(jnp.int32, (1, depth), 1)
        source = lane // (2 * per_source)
        inner = lane - source * (2 * per_source)
        part = inner // per_source
        local = inner - part * per_source
        pair = source * (per_source // 2) + local // 2
        wave = jnp.where(local % 2 == 0, pair, waves - 1 - pair)
        weight = jnp.where(wave == 0, 1.0, 2.0).astype(F32)
        wave_f = wave.astype(F32)
        shift = part.astype(F32) * (NLON // 4)
        for c in range(0, cols, 64):
            turns = longitude[c : c + 64] * wave_f + shift
            turns = turns - jnp.floor(turns * (1.0 / NLON) + 0.5) * NLON
            table_s[c : c + 64, :] = (weight * cosine(turns * (1.0 / NLON))).astype(BF16)

    block = coeff_ref[...]
    products = dot(table_s[...], block.reshape(depth, block.shape[2]))
    row = row_s[...]
    main = jnp.zeros((cols, LANES), F32)
    rest = jnp.zeros((cols, LANES), F32)
    last = products[:, 4 * LANES :]
    for r in range(4):
        main = jnp.where(row == r, products[:, r * LANES : (r + 1) * LANES], main)
        moved = last if r == 0 else pltpu.roll(last, LANES - SLOT_LANES * r, 1)
        rest = jnp.where(row == r, moved, rest)
    state_s[v] = main.astype(BF16)
    state_s[4 + v] = rest.astype(BF16)

    @pl.when(v == pl.num_programs(0) - 1)
    def _():
        hits = lax.broadcasted_iota(jnp.int32, (LANES, cols), 0) == owner_ref[...]
        hits_f = jnp.where(hits, 1.0, 0.0).astype(F32)
        before = (
            lax.broadcasted_iota(jnp.int32, (cols, cols), 0)
            < lax.broadcasted_iota(jnp.int32, (cols, cols), 1)
        )
        earlier = dot(hits_f.astype(BF16), jnp.where(before, 1.0, 0.0).astype(BF16))
        first = (lax.broadcasted_iota(jnp.int32, (LANES, cols), 0) * slots).astype(F32)
        spot = jnp.sum(hits_f * (first + earlier), axis=0, keepdims=True).astype(jnp.int32)
        spot_ref[...] = spot
        place = lax.broadcasted_iota(jnp.int32, (slots * LANES, cols), 0) == spot
        place = jnp.where(place, 1.0, 0.0).astype(BF16)
        lane = lax.broadcasted_iota(jnp.int32, (1, LANES), 1)
        tail = jnp.zeros((cols, LANES), F32)
        for u in range(4):
            out_ref[:, u * LANES : (u + 1) * LANES] = dot(place, state_s[u]).astype(BF16)
            part = state_s[4 + u].astype(F32)
            part = part if u == 0 else pltpu.roll(part, SLOT_LANES * u, 1)
            tail = jnp.where(lane // SLOT_LANES == u, part, tail)
        out_ref[:, 4 * LANES :] = dot(place, tail.astype(BF16)).astype(BF16)


def column_states(coeff, index, owner, slots):
    sources, rows, lanes = coeff.shape
    cols = index.shape[1]
    total = slots * LANES
    return pl.pallas_call(
        state_kernel,
        out_shape=(
            jax.ShapeDtypeStruct((total, lanes), BF16),
            jax.ShapeDtypeStruct((1, cols), jnp.int32),
        ),
        grid=(4,),
        in_specs=[
            pl.BlockSpec((1, cols), lambda v: (0, 0)),
            pl.BlockSpec((1, cols), lambda v: (0, 0)),
            pl.BlockSpec((sources, rows // 4, lanes), lambda v: (0, v, 0)),
        ],
        out_specs=(
            pl.BlockSpec((total, lanes), lambda v: (0, 0)),
            pl.BlockSpec((1, cols), lambda v: (0, 0)),
        ),
        scratch_shapes=[
            pltpu.VMEM((cols, sources * rows // 4), BF16),
            pltpu.VMEM((cols, LANES), F32),
            pltpu.VMEM((8, cols, LANES), BF16),
        ],
        name="states",
    )(index, owner, coeff)


def answer_kernel(state_ref, jac_ref, bias_ref, out_ref, jac_s):
    channels = jac_ref.shape[1]
    levels = jac_ref.shape[0] // 4
    rest = levels - LANES

    @pl.when(pl.program_id(0) == 0)
    def _():
        jac = jac_ref[...].astype(F32)
        jac_s[...] = jnp.zeros_like(jac_s)
        for v in range(4):
            at = v * levels
            jac_s[v * LANES : (v + 1) * LANES, :] = jac[at : at + LANES].astype(BF16)
            lo = 4 * LANES + v * SLOT_LANES
            piece = jnp.concatenate(
                [jac[at + LANES : at + levels], jnp.zeros((16 - rest, channels), F32)], axis=0
            )
            jac_s[lo : lo + 16, :] = piece.astype(BF16)

    depart = dot(state_ref[...], jac_s[...]) + bias_ref[...]
    weighted = (depart / jnp.sqrt(1.0 + depart * depart * 0.25)).astype(BF16)
    out_ref[:, :channels] = depart.astype(BF16)
    out_ref[:, 3 * LANES : 3 * LANES + jac_ref.shape[0]] = lax.dot_general(
        weighted, jac_ref[...], (((1,), (1,)), ((), ())), preferred_element_type=F32
    ).astype(BF16)


def answers(states, jac_t, bias):
    total, lanes = states.shape
    width, channels = jac_t.shape
    out_lanes = -(-channels // LANES) * LANES + -(-width // LANES) * LANES
    steps = 2
    return pl.pallas_call(
        answer_kernel,
        out_shape=jax.ShapeDtypeStruct((total, out_lanes), BF16),
        grid=(steps,),
        in_specs=[
            pl.BlockSpec((total // steps, lanes), lambda g: (g, 0)),
            pl.BlockSpec((width, channels), lambda g: (0, 0)),
            pl.BlockSpec((1, channels), lambda g: (0, 0)),
        ],
        out_specs=pl.BlockSpec((total // steps, out_lanes), lambda g: (g, 0)),
        scratch_shapes=[pltpu.VMEM((lanes, channels), BF16)],
        name="answers",
    )(states, jac_t, bias)


def collect_kernel(spot_ref, back_ref, depart_ref, grad_ref):
    cols = spot_ref.shape[1]
    total = back_ref.shape[0]
    spot = jnp.transpose(jnp.broadcast_to(spot_ref[...].astype(F32), (LANES, cols)))[:, :1]
    place = lax.broadcasted_iota(jnp.int32, (cols, total), 1) == spot.astype(jnp.int32)
    place = jnp.where(place, 1.0, 0.0).astype(BF16)
    channels = depart_ref.shape[0]
    width = grad_ref.shape[0]
    depart = jnp.transpose(dot(place, back_ref[:, : 3 * LANES]))
    depart_ref[...] = depart[:channels].astype(BF16)
    grad = jnp.transpose(dot(place, back_ref[:, 3 * LANES :]))
    grad_ref[...] = grad[:width].astype(BF16)


def collect(spot, back, channels, width):
    cols = spot.shape[1]
    return pl.pallas_call(
        collect_kernel,
        out_shape=(
            jax.ShapeDtypeStruct((channels, cols), BF16),
            jax.ShapeDtypeStruct((width, cols), BF16),
        ),
        name="collect",
    )(spot, back)


def exchange(x):
    return lax.all_to_all(x, ("wave", "lat"), split_axis=0, concat_axis=0, tiled=True)


def local(control, spread, vertical, legendre, column_index, column_owner, jacobian, channel_bias):
    pairs = control.shape[0]
    wave_count = lax.axis_size("wave")
    device_count = wave_count * lax.axis_size("lat")
    cols = column_index.shape[0]
    slots = max(2, 2 * cols // device_count)
    var = lax.axis_index("lat") // 2
    pair_base = (lax.axis_index("wave") * pairs).astype(jnp.int32).reshape(1)
    blocks = fourier_blocks(control, spread[var], vertical[var], legendre, pair_base, device_count)
    coeff = exchange(blocks)
    coeff = coeff.reshape(wave_count, -1, coeff.shape[2])
    outgoing, spot = column_states(
        coeff, column_index.reshape(1, cols), column_owner.reshape(1, cols), slots
    )
    lanes = outgoing.shape[1]
    states = exchange(outgoing.reshape(device_count, slots, lanes))
    jac_t = jnp.transpose(jacobian[0])
    reply = answers(states.reshape(device_count * slots, lanes), jac_t, channel_bias)
    back = exchange(reply.reshape(device_count, slots, reply.shape[1]))
    departures, increments = collect(
        spot, back.reshape(device_count * slots, -1), jac_t.shape[1], jac_t.shape[0]
    )
    return (jnp.transpose(departures), jnp.transpose(increments))


def solution(mesh):
    return jax.shard_map(
        local,
        mesh=mesh,
        in_specs=(
            P("wave", None, "lat", None),
            P(),
            P(),
            P("wave", None, None),
            P(("wave", "lat")),
            P(("wave", "lat"), None),
            P(("wave", "lat"), None, None),
            P(("wave", "lat"), None),
        ),
        out_specs=(P(("wave", "lat"), None), P(("wave", "lat"), None)),
        check_vma=False,
    )
```

profile of v0, /device:TPU:1, one launch (start us, length us, event | category | flops | bytes accessed | tf_op | source)
XLA Modules:
  0.0 197.6 jit_solution(911677599806789224)
XLA Ops:
  0.6 0.0 copy-start
  0.7 1.2 constant_dynamic-slice_fusion
  1.9 0.2 copy-done
  2.1 0.3 constant_dynamic-slice_fusion.1
  2.4 0.6 pad.9.vert_ref
  3.1 0.8 pad.8.spread_ref
  3.9 18.1 %fourier.1 = bf16[128,40,640]{2,1,0:T(8,128)(2,1)} custom-call(s32[1]{0:T(128)} %bitcast.2.base_ref, bf16[20,1,137,641]{3,2,1,0:T(8,128)(2,1)} %bitcast.26, f32[137,768]{1,0:T(8,128)} %pad.8.spread_ref, bf16[144,137]{1,0:T(8,128)(2,1)} %pad.9.vert_ref, bf16[20,641,512]{2,1,0:T(8,128)(2,1)} %leg_ref.1), custom_call_target="tpu_custom_call" | custom-call | tf_op jit(solution)/shard_map/fourier/pallas_call | solution.py:78
  22.0 89.8 %all_to_all.15 = bf16[128,40,640]{2,1,0:T(8,128)(2,1)} all-to-all(bf16[128,40,640]{2,1,0:T(8,128)(2,1)} %fourier.1), channel_id=1, replica_groups=mesh['wave'=16,'lat'=8] {'wave','lat'}, dimensions={0} | all-to-all | bytes 13107200 | tf_op jit(solution)/shard_map/all_to_all | solution.py:279
  111.8 12.1 %states.1 = (bf16[1024,640]{1,0:T(8,128)(2,1)}, s32[1,512]{1,0:T(1,128)}) custom-call(s32[1,512]{1,0:T(1,128)} %bitcast.31, s32[1,512]{1,0:T(1,128)} %bitcast.32, bf16[16,320,640]{2,1,0:T(8,128)(2,1)} %bitcast.22), custom_call_target="tpu_custom_call" | custom-call | tf_op jit(solution)/shard_map/states/pallas_call | solution.py:181
  123.9 28.4 %all_to_all.16 = bf16[128,8,640]{2,1,0:T(8,128)(2,1)} all-to-all(bf16[128,8,640]{2,1,0:T(8,128)(2,1)} %bitcast.28), channel_id=1, replica_groups=mesh['wave'=16,'lat'=8] {'wave','lat'}, dimensions={0} | all-to-all | bytes 2621440 | tf_op jit(solution)/shard_map/all_to_all | solution.py:279
  152.3 4.8 %answers.1 = bf16[1024,1024]{1,0:T(8,128)(2,1)} custom-call(bf16[1024,640]{1,0:T(8,128)(2,1)} %bitcast.25, bf16[548,366]{1,0:T(8,128)(2,1)} %bitcast.29, f32[1,366]{1,0:T(1,128)} %bias_ref.1), custom_call_target="tpu_custom_call" | custom-call | tf_op jit(solution)/shard_map/answers/pallas_call | solution.py:237
  157.1 36.2 %all_to_all.17 = bf16[128,8,1024]{2,1,0:T(8,128)(2,1)} all-to-all(bf16[128,8,1024]{2,1,0:T(8,128)(2,1)} %bitcast.23), channel_id=1, replica_groups=mesh['wave'=16,'lat'=8] {'wave','lat'}, dimensions={0} | all-to-all | bytes 4194304 | tf_op jit(solution)/shard_map/all_to_all | solution.py:279
  193.3 4.3 %collect.1 = (bf16[366,512]{1,0:T(8,128)(2,1)}, bf16[548,512]{1,0:T(8,128)(2,1)}) custom-call(s32[1,512]{1,0:T(1,128)} %get-tuple-element.6.spot_ref, bf16[1024,1024]{1,0:T(8,128)(2,1)} %bitcast.24), custom_call_target="tpu_custom_call" | custom-call | tf_op jit(solution)/shard_map/collect/pallas_call | solution.py:268
  (2 shorter events, 0.0 us)
Async XLA Ops:
  0.6 1.4 copy-start
where the time goes:
time: 198 us
  blocking collectives  154 us (78%)
  Pallas kernels  39.4 us (20%)
  local copies, waits for them, and re-layouts  3.17 us (2%)
    all_to_all x3, blocking collectives, exchange(): lax.all_to_all(x, ('wave', 'lat'), split_axis=0, concat_axis=0, tiled=True)  154 us
    pallas_call x1, Pallas kernels, fourier_blocks(): pl.pallas_call(fourier_kernel, out_shape=jax.ShapeDtypeStruct((dests, 2 *...  18.1 us
    pallas_call x1, Pallas kernels, column_states(): pl.pallas_call(state_kernel, out_shape=(jax.ShapeDtypeStruct((total, lane...  12.1 us
    pallas_call x1, Pallas kernels, answers(): pl.pallas_call(answer_kernel, out_shape=jax.ShapeDtypeStruct((total, out_...  4.83 us
    pallas_call x1, Pallas kernels, collect(): pl.pallas_call(collect_kernel, out_shape=(jax.ShapeDtypeStruct((channels,...  4.33 us

commit v1 on v0

v1 whole, which is shorter than its diff:
```python
import functools
import math

import jax
import jax.numpy as jnp
from jax import lax
from jax.experimental import pallas as pl
from jax.experimental.pallas import tpu as pltpu
from jax.sharding import PartitionSpec as P

NLON = 2560
LANES = 128
SLOT_LANES = 32
REST = 12
GROUP = 10
F32 = jnp.float32
BF16 = jnp.bfloat16


def dot(a, b):
    return jnp.dot(a, b, preferred_element_type=F32)


def fourier_kernel(base_ref, ctrl_ref, spread_ref, vert_ref, leg_ref, out_ref, main_s, rem_s):
    slots = ctrl_ref.shape[3]
    waves = slots - 1
    rows = leg_ref.shape[2]
    dests = out_ref.shape[0]
    steps = pl.num_programs(0) - 1
    g = pl.program_id(0)

    @pl.when(g == 0)
    def _():
        rem_s[...] = jnp.zeros_like(rem_s)

    @pl.when(g < steps)
    def _():
        spread = spread_ref[...]
        lane = lax.broadcasted_iota(jnp.int32, (1, waves), 1)
        slot = lax.broadcasted_iota(jnp.int32, (1, slots), 1)
        second_scale = pltpu.roll(spread, 1, 1)
        pair0 = base_ref[0] + g * 4
        rests = []
        for i in range(4):
            pair = pair0 + i
            first_scale = pltpu.roll(spread, waves - pair, 1)
            scale = jnp.where(lane < waves - pair, first_scale, second_scale)
            scale = jnp.concatenate([scale, spread[:, waves - 1 :]], axis=1)
            scaled = (ctrl_ref[i, 0].astype(F32) * scale).astype(BF16)
            spec = dot(vert_ref[...], scaled).astype(BF16)
            keep = slot < waves - pair
            zero = jnp.zeros_like(spec)
            first = jnp.where(keep, spec, zero)
            second = jnp.where(keep, zero, spec)
            both = jnp.concatenate([first[:, 256:], second[:, 256:]], axis=0)
            sums = dot(both, leg_ref[i, 256:, :])
            half_rows = spec.shape[0]
            parts = (sums[:half_rows] + dot(first[:, :256], leg_ref[i, :256, :]), sums[half_rows:])
            for h in range(2):
                j = 2 * i + h
                main_s[pl.ds(j, rows, stride=8), :] = jnp.transpose(parts[h][:LANES])
                rests.append(parts[h][LANES : LANES + REST])
        out_ref[...] = main_s[...].reshape(dests, 32, LANES).astype(BF16)
        for step in range(5):

            @pl.when(g == step)
            def _():
                for j in range(8):
                    k = 8 * step + j
                    at = LANES * (k // GROUP) + REST * (k % GROUP)
                    rem_s[at : at + REST, :] = rests[j]

    @pl.when(g == steps)
    def _():
        for u in range(4):
            main_s[pl.ds(u, rows, stride=4), :] = jnp.transpose(rem_s[u * LANES : (u + 1) * LANES])
        out_ref[:, :16, :] = main_s[: 4 * rows, :].reshape(dests, 16, LANES).astype(BF16)


def fourier_blocks(control, spread, vertical, legendre, pair_base, dests):
    pairs, slots, _, modes = control.shape
    rows = legendre.shape[2]
    ctrl = jnp.transpose(control, (0, 2, 3, 1))
    vert = jnp.pad(vertical, ((0, 144 - vertical.shape[0]), (0, 0)))
    steps = pairs // 4
    return pl.pallas_call(
        fourier_kernel,
        out_shape=jax.ShapeDtypeStruct((dests, 32 * steps + 16, LANES), BF16),
        grid=(steps + 1,),
        in_specs=[
            pl.BlockSpec(memory_space=pltpu.SMEM),
            pl.BlockSpec((4, 1, modes, slots), lambda g: (jnp.minimum(g, steps - 1), 0, 0, 0)),
            pl.BlockSpec((modes, slots - 1), lambda g: (0, 0)),
            pl.BlockSpec((144, modes), lambda g: (0, 0)),
            pl.BlockSpec((4, slots, rows), lambda g: (jnp.minimum(g, steps - 1), 0, 0)),
        ],
        out_specs=pl.BlockSpec((dests, 32, LANES), lambda g: (0, g, 0)),
        scratch_shapes=[pltpu.VMEM((rows * 8, LANES), F32), pltpu.VMEM((4 * LANES, rows), F32)],
        name="fourier",
    )(pair_base, ctrl, jnp.transpose(spread), vert, legendre)


def cosine(turns):
    x = turns * math.pi
    y = x * x
    s = -1.0 / 39916800.0
    for c in (1.0 / 362880.0, -1.0 / 5040.0, 1.0 / 120.0, -1.0 / 6.0, 1.0):
        s = s * y + c
    s = s * x
    return 1.0 - 2.0 * (s * s)


def table_kernel(index_ref, owner_ref, main_ref, rest_ref, place_ref, row_ref, spot_ref):
    cols = index_ref.shape[1]
    depth = main_ref.shape[1]
    waves = depth // 2
    slots = place_ref.shape[0] // LANES
    column = jnp.transpose(jnp.broadcast_to(index_ref[...].astype(F32), (LANES, cols)))[:, :1]
    row = jnp.floor((column + 0.5) * (1.0 / NLON))
    longitude = column - row * NLON
    row_ref[...] = jnp.broadcast_to(row, row_ref.shape)
    lane = lax.broadcasted_iota(jnp.int32, (1, depth), 1)

    def fill(ref, source, part, local):
        pair = source * 20 + local // 2
        wave = jnp.where(local % 2 == 0, pair, waves - 1 - pair)
        weight = jnp.where(wave == 0, 1.0, 2.0).astype(F32)
        wave_f = wave.astype(F32)
        shift = part.astype(F32) * (NLON // 4)
        for c in range(0, cols, 64):
            turns = longitude[c : c + 64] * wave_f + shift
            turns = turns - jnp.floor(turns * (1.0 / NLON) + 0.5) * NLON
            ref[c : c + 64, :] = (weight * cosine(turns * (1.0 / NLON))).astype(BF16)

    inner = lane % 80
    fill(main_ref, lane // 80, inner // 40, inner % 40)
    inner = lane % 128
    fill(rest_ref, inner % 32 // 2, inner % 2, inner // 32 * GROUP + lane // 128)

    hits = lax.broadcasted_iota(jnp.int32, (LANES, cols), 0) == owner_ref[...]
    hits_f = jnp.where(hits, 1.0, 0.0).astype(F32)
    before = (
        lax.broadcasted_iota(jnp.int32, (cols, cols), 0)
        < lax.broadcasted_iota(jnp.int32, (cols, cols), 1)
    )
    earlier = dot(hits_f.astype(BF16), jnp.where(before, 1.0, 0.0).astype(BF16))
    first = (lax.broadcasted_iota(jnp.int32, (LANES, cols), 0) * slots).astype(F32)
    spot = jnp.sum(hits_f * (first + earlier), axis=0, keepdims=True).astype(jnp.int32)
    spot_ref[...] = spot
    place = lax.broadcasted_iota(jnp.int32, (slots * LANES, cols), 0) == spot
    place_ref[...] = jnp.where(place, 1.0, 0.0).astype(BF16)


def tables(index, owner, depth, slots):
    cols = index.shape[1]
    return pl.pallas_call(
        table_kernel,
        out_shape=(
            jax.ShapeDtypeStruct((cols, depth), BF16),
            jax.ShapeDtypeStruct((cols, depth), BF16),
            jax.ShapeDtypeStruct((slots * LANES, cols), BF16),
            jax.ShapeDtypeStruct((cols, LANES), F32),
            jax.ShapeDtypeStruct((1, cols), jnp.int32),
        ),
        cost_estimate=pl.CostEstimate(
            flops=60 * cols * depth, bytes_accessed=4 << 20, transcendentals=0
        ),
        name="tables",
    )(index, owner)


def state_kernel(
    main_ref, rest_ref, place_ref, row_ref, coeff_ref, out_ref, coeff_s, tail_s, take_s, state_s
):
    v = pl.program_id(0)
    cols = main_ref.shape[0]
    depth = main_ref.shape[1]
    sources = coeff_ref.shape[0]
    block = coeff_ref[...].astype(F32).reshape(sources * 2, 22, 8, LANES)
    for r in range(4):
        picked = jnp.stack([block[:, 4 * g + r] for g in range(5)], axis=1)
        coeff_s[:, r * LANES : (r + 1) * LANES] = picked.reshape(depth, LANES).astype(BF16)
    take_s[...] = block[:, 20:].reshape(sources * 2 * 16, LANES)
    lane = lax.broadcasted_iota(jnp.int32, (1, LANES), 1)
    odd = v % 2
    tile = v // 2
    for u in range(4):
        picked = [take_s[pl.ds(4 * r + u, sources * 2, stride=16), :] for r in range(4)]
        for k in range(GROUP):
            at = (k * 4 + u) * sources * 2
            kept = tail_s[tile, at : at + sources * 2, :]
            for r in range(4):
                moved = pltpu.roll(picked[r], (64 * odd + 16 * r - REST * k + LANES) % LANES, 1)
                kept = jnp.where(lane // 16 == 4 * odd + r, moved, kept)
            tail_s[tile, at : at + sources * 2, :] = kept
    row = row_ref[...]
    products = dot(main_ref[...], coeff_s[...])
    main = products[:, :LANES]
    for r in range(1, 4):
        main = jnp.where(row == r, products[:, r * LANES : (r + 1) * LANES], main)
    state_s[v] = main.astype(BF16)

    @pl.when(v == pl.num_programs(0) - 1)
    def _():
        place = place_ref[...]
        tail = jnp.zeros((cols, LANES), F32)
        for half in range(2):
            products = dot(rest_ref[...], tail_s[half].astype(BF16))
            for slot in range(8):
                u = 2 * half + slot // 4
                shift = (SLOT_LANES * u - 16 * slot) % LANES
                moved = products if shift == 0 else pltpu.roll(products, shift, 1)
                hit = (row == slot % 4) & (lane // SLOT_LANES == u) & (lane % SLOT_LANES < 9)
                tail = jnp.where(hit, moved, tail)
        for u in range(4):
            out_ref[:, u * LANES : (u + 1) * LANES] = dot(place, state_s[u]).astype(BF16)
        out_ref[:, 4 * LANES :] = dot(place, tail.astype(BF16)).astype(BF16)


def column_states(coeff, main_table, rest_table, place, row):
    sources, rows, _ = coeff.shape
    cols, depth = main_table.shape
    total = place.shape[0]
    whole = lambda x: pl.BlockSpec(x.shape, lambda v: (0,) * x.ndim)
    return pl.pallas_call(
        state_kernel,
        out_shape=jax.ShapeDtypeStruct((total, 5 * LANES), BF16),
        grid=(4,),
        in_specs=[
            whole(main_table),
            whole(rest_table),
            whole(place),
            whole(row),
            pl.BlockSpec((sources, rows // 4, LANES), lambda v: (0, v, 0)),
        ],
        out_specs=pl.BlockSpec((total, 5 * LANES), lambda v: (0, 0)),
        scratch_shapes=[
            pltpu.VMEM((depth, 4 * LANES), BF16),
            pltpu.VMEM((2, depth, LANES), F32),
            pltpu.VMEM((sources * 2 * 16, LANES), F32),
            pltpu.VMEM((4, cols, LANES), BF16),
        ],
        name="states",
    )(main_table, rest_table, place, row, coeff)


def answer_kernel(state_ref, jac_ref, bias_ref, out_ref, jac_s):
    channels = jac_ref.shape[1]
    levels = jac_ref.shape[0] // 4
    rest = levels - LANES

    @pl.when(pl.program_id(0) == 0)
    def _():
        jac = jac_ref[...].astype(F32)
        jac_s[...] = jnp.zeros_like(jac_s)
        for v in range(4):
            at = v * levels
            jac_s[v * LANES : (v + 1) * LANES, :] = jac[at : at + LANES].astype(BF16)
            lo = 4 * LANES + v * SLOT_LANES
            piece = jnp.concatenate(
                [jac[at + LANES : at + levels], jnp.zeros((16 - rest, channels), F32)], axis=0
            )
            jac_s[lo : lo + 16, :] = piece.astype(BF16)

    depart = dot(state_ref[...], jac_s[...]) + bias_ref[...]
    weighted = (depart / jnp.sqrt(1.0 + depart * depart * 0.25)).astype(BF16)
    out_ref[:, :channels] = depart.astype(BF16)
    out_ref[:, 3 * LANES : 3 * LANES + jac_ref.shape[0]] = lax.dot_general(
        weighted, jac_ref[...], (((1,), (1,)), ((), ())), preferred_element_type=F32
    ).astype(BF16)


def answers(states, jac_t, bias):
    total, lanes = states.shape
    width, channels = jac_t.shape
    out_lanes = -(-channels // LANES) * LANES + -(-width // LANES) * LANES
    steps = 2
    return pl.pallas_call(
        answer_kernel,
        out_shape=jax.ShapeDtypeStruct((total, out_lanes), BF16),
        grid=(steps,),
        in_specs=[
            pl.BlockSpec((total // steps, lanes), lambda g: (g, 0)),
            pl.BlockSpec((width, channels), lambda g: (0, 0)),
            pl.BlockSpec((1, channels), lambda g: (0, 0)),
        ],
        out_specs=pl.BlockSpec((total // steps, out_lanes), lambda g: (g, 0)),
        scratch_shapes=[pltpu.VMEM((lanes, channels), BF16)],
        name="answers",
    )(states, jac_t, bias)


def collect_kernel(spot_ref, back_ref, depart_ref, grad_ref):
    cols = spot_ref.shape[1]
    total = back_ref.shape[0]
    spot = jnp.transpose(jnp.broadcast_to(spot_ref[...].astype(F32), (LANES, cols)))[:, :1]
    place = lax.broadcasted_iota(jnp.int32, (cols, total), 1) == spot.astype(jnp.int32)
    place = jnp.where(place, 1.0, 0.0).astype(BF16)
    channels = depart_ref.shape[0]
    width = grad_ref.shape[0]
    depart = jnp.transpose(dot(place, back_ref[:, : 3 * LANES]))
    depart_ref[...] = depart[:channels].astype(BF16)
    grad = jnp.transpose(dot(place, back_ref[:, 3 * LANES :]))
    grad_ref[...] = grad[:width].astype(BF16)


def collect(spot, back, channels, width):
    cols = spot.shape[1]
    return pl.pallas_call(
        collect_kernel,
        out_shape=(
            jax.ShapeDtypeStruct((channels, cols), BF16),
            jax.ShapeDtypeStruct((width, cols), BF16),
        ),
        name="collect",
    )(spot, back)


def exchange(x):
    return lax.all_to_all(x, ("wave", "lat"), split_axis=0, concat_axis=0, tiled=True)


def local(control, spread, vertical, legendre, column_index, column_owner, jacobian, channel_bias):
    pairs = control.shape[0]
    wave_count = lax.axis_size("wave")
    device_count = wave_count * lax.axis_size("lat")
    cols = column_index.shape[0]
    slots = max(2, 2 * cols // device_count)
    var = lax.axis_index("lat") // 2
    pair_base = (lax.axis_index("wave") * pairs).astype(jnp.int32).reshape(1)
    blocks = fourier_blocks(control, spread[var], vertical[var], legendre, pair_base, device_count)
    main_table, rest_table, place, row, spot = tables(
        column_index.reshape(1, cols), column_owner.reshape(1, cols), 4 * pairs * wave_count, slots
    )
    coeff = exchange(blocks).reshape(wave_count, -1, LANES)
    outgoing = column_states(coeff, main_table, rest_table, place, row)
    lanes = outgoing.shape[1]
    states = exchange(outgoing.reshape(device_count, slots, lanes))
    jac_t = jnp.transpose(jacobian[0])
    reply = answers(states.reshape(device_count * slots, lanes), jac_t, channel_bias)
    back = exchange(reply.reshape(device_count, slots, reply.shape[1]))
    departures, increments = collect(
        spot, back.reshape(device_count * slots, -1), jac_t.shape[1], jac_t.shape[0]
    )
    return (jnp.transpose(departures), jnp.transpose(increments))


def solution(mesh):
    return jax.shard_map(
        local,
        mesh=mesh,
        in_specs=(
            P("wave", None, "lat", None),
            P(),
            P(),
            P("wave", None, None),
            P(("wave", "lat")),
            P(("wave", "lat"), None),
            P(("wave", "lat"), None, None),
            P(("wave", "lat"), None),
        ),
        out_specs=(P(("wave", "lat"), None), P(("wave", "lat"), None)),
        check_vma=False,
    )
```

time: 198 us -> 187 us (0.944)
  blocking collectives: 154 us -> 65.8 us
  waiting for transfers between devices: 0 us -> 61.7 us
  starting transfers between devices: 0 us -> 11.9 us
  Pallas kernels: 39.4 us -> 42 us
    all_to_all x3 -> x2, blocking collectives: 154 us -> 65.8 us  [exchange(): lax.all_to_all(x, ('wave', 'lat'), split_axis=0, concat_axis=0, tiled=True)]
    all_to_all x0 -> x1, waiting for transfers between devices: none -> 61.7 us  [exchange(): lax.all_to_all(x, ('wave', 'lat'), split_axis=0, concat_axis=0, tiled=True)]
    all_to_all x0 -> x1, starting transfers between devices: none -> 11.9 us  [exchange(): lax.all_to_all(x, ('wave', 'lat'), split_axis=0, concat_axis=0, tiled=True)]
    pallas_call x2 -> x3, Pallas kernels: 30.3 us -> 32.9 us  [the longest x1 14.5 us: fourier_blocks(): pl.pallas_call(fourier_kernel, out_shape=jax.ShapeDtypeStruct((dests, 32...]
  transfers between devices with their start and end apart: 0 -> 1, of which waited for: 0 -> 1; matrix products, arithmetic and copies ran while one was open for 0% -> 0% of each run, Pallas kernels for 0% -> 4%
where the time goes in v1:
time: 187 us; the launch traced here: 186 us
  blocking collectives  65.8 us (35%)
  waiting for transfers between devices  61.7 us (33%)
  Pallas kernels  42 us (22%)
  starting transfers between devices  11.9 us (6%)
  local copies, waits for them, and re-layouts  4.16 us (2%)
    all_to_all x2, blocking collectives, exchange(): lax.all_to_all(x, ('wave', 'lat'), split_axis=0, concat_axis=0, tiled=True)  65.8 us
    all_to_all x1, waiting for transfers between devices, exchange(): lax.all_to_all(x, ('wave', 'lat'), split_axis=0, concat_axis=0, tiled=True)  61.7 us
    pallas_call x1, Pallas kernels, fourier_blocks(): pl.pallas_call(fourier_kernel, out_shape=jax.ShapeDtypeStruct((dests, 32...  14.5 us
    all_to_all x1, starting transfers between devices, exchange(): lax.all_to_all(x, ('wave', 'lat'), split_axis=0, concat_axis=0, tiled=True)  11.9 us
    pallas_call x1, Pallas kernels, column_states(): pl.pallas_call(state_kernel, out_shape=jax.ShapeDtypeStruct((total, 5 * L...  10.5 us
    pallas_call x1, Pallas kernels, tables(): pl.pallas_call(table_kernel, out_shape=(jax.ShapeDtypeStruct((cols, depth...  7.87 us
    pallas_call x1, Pallas kernels, answers(): pl.pallas_call(answer_kernel, out_shape=jax.ShapeDtypeStruct((total, out_...  4.82 us
    pallas_call x1, Pallas kernels, collect(): pl.pallas_call(collect_kernel, out_shape=(jax.ShapeDtypeStruct((channels,...  4.33 us
  transfers between devices with their start and end apart: 1, of which 1 were waited for; matrix products, arithmetic and copies ran while one was open for 0% of the time, Pallas kernels for 4%

profile of v1, /device:TPU:1, one launch (start us, length us, event | category | flops | bytes accessed | tf_op | source)
XLA Modules:
  0.0 186.2 jit_solution(3213047619467210764)
XLA Ops:
  0.6 0.0 copy-start
  0.7 1.3 copy-done
  2.0 0.3 constant_dynamic-slice_fusion.1
  2.3 0.8 copy.16
  3.1 1.1 constant_dynamic-slice_fusion
  4.2 0.6 pad.4.vert_ref
  4.8 14.5 %fourier.1 = bf16[128,176,128]{2,1,0:T(8,128)(2,1)} custom-call(s32[1]{0:T(128)} %bitcast.2.base_ref, bf16[20,1,137,641]{3,2,1,0:T(8,128)(2,1)} %bitcast.26, f32[137,640]{1,0:T(8,128)} %bitcast.27, bf16[144,137]{1,0:T(8,128)(2,1)} %pad.4.vert_ref, bf16[20,641,512]{2,1,0:T(8,128)(2,1)} %leg_ref.1), custom_call_target="tpu_custom_call" | custom-call | tf_op jit(solution)/shard_map/fourier/pallas_call | solution.py:86
  19.4 11.9 %all-to-all-start = ((bf16[128,176,128]{2,1,0:T(8,128)(2,1)}), bf16[128,176,128]{2,1,0:T(8,128)(2,1)}, u32[]{:S(2)}, u32[]{:S(2)}) async-start(bf16[128,176,128]{2,1,0:T(8,128)(2,1)} %fourier.1), calls=%async_computation | async-start | bytes 11534336 | tf_op jit(solution)/shard_map/all_to_all | solution.py:320
  31.3 7.9 %tables.1 = (bf16[512,1280]{1,0:T(8,128)(2,1)}, bf16[512,1280]{1,0:T(8,128)(2,1)}, bf16[1024,512]{1,0:T(8,128)(2,1)}, f32[512,128]{1,0:T(8,128)}, s32[1,512]{1,0:T(1,128)}) custom-call(s32[1,512]{1,0:T(1,128)} %bitcast.32, s32[1,512]{1,0:T(1,128)} %bitcast.33), custom_call_target="tpu_custom_call" | custom-call | flops 39321600 | bytes 4194304 | tf_op jit(solution)/shard_map/tables/pallas_call | solution.py:156
  39.1 61.7 %all-to-all-done = bf16[128,176,128]{2,1,0:T(8,128)(2,1)} async-done(((bf16[128,176,128]{2,1,0:T(8,128)(2,1)}), bf16[128,176,128]{2,1,0:T(8,128)(2,1)}, u32[]{:S(2)}, u32[]{:S(2)}) %all-to-all-start) | async-done | bytes 5767200 | tf_op jit(solution)/shard_map/all_to_all | solution.py:320
  100.8 10.5 %states.1 = bf16[1024,640]{1,0:T(8,128)(2,1)} custom-call(bf16[512,1280]{1,0:T(8,128)(2,1)} %get-tuple-element.10.main_ref, bf16[512,1280]{1,0:T(8,128)(2,1)} %get-tuple-element.11.rest_ref, bf16[1024,512]{1,0:T(8,128)(2,1)} %get-tuple-element.12.place_ref, f32[512,128]{1,0:T(8,128)} %get-tuple-element.13.row_ref, bf16[16,1408,128]{2,1,0:T(8,128)(2,1)} %bitcast.7.coeff_ref), custom_call_target="tpu_custom_call" | custom-call | tf_op jit(solution)/shard_map/states/pallas_call | solution.py:225
  111.3 29.6 %all_to_all.15 = bf16[128,8,640]{2,1,0:T(8,128)(2,1)} all-to-all(bf16[128,8,640]{2,1,0:T(8,128)(2,1)} %bitcast.25), channel_id=1, replica_groups=mesh['wave'=16,'lat'=8] {'wave','lat'}, dimensions={0} | all-to-all | bytes 2621440 | tf_op jit(solution)/shard_map/all_to_all | solution.py:320
  140.9 4.8 %answers.1 = bf16[1024,1024]{1,0:T(8,128)(2,1)} custom-call(bf16[1024,640]{1,0:T(8,128)(2,1)} %bitcast.24, bf16[548,366]{1,0:T(8,128)(2,1)} %bitcast.28, f32[1,366]{1,0:T(1,128)} %bias_ref.1), custom_call_target="tpu_custom_call" | custom-call | tf_op jit(solution)/shard_map/answers/pallas_call | solution.py:278
  145.7 36.2 %all_to_all.16 = bf16[128,8,1024]{2,1,0:T(8,128)(2,1)} all-to-all(bf16[128,8,1024]{2,1,0:T(8,128)(2,1)} %bitcast.22), channel_id=1, replica_groups=mesh['wave'=16,'lat'=8] {'wave','lat'}, dimensions={0} | all-to-all | bytes 4194304 | tf_op jit(solution)/shard_map/all_to_all | solution.py:320
  181.9 4.3 %collect.1 = (bf16[366,512]{1,0:T(8,128)(2,1)}, bf16[548,512]{1,0:T(8,128)(2,1)}) custom-call(s32[1,512]{1,0:T(1,128)} %get-tuple-element.9.spot_ref, bf16[1024,1024]{1,0:T(8,128)(2,1)} %bitcast.23), custom_call_target="tpu_custom_call" | custom-call | tf_op jit(solution)/shard_map/collect/pallas_call | solution.py:309
  (1 shorter events, 0.0 us)
Async XLA Ops:
  0.6 1.4 copy-start
  19.4 81.5 %all-to-all-start = ((bf16[128,176,128]{2,1,0:T(8,128)(2,1)}), bf16[128,176,128]{2,1,0:T(8,128)(2,1)}, u32[]{:S(2)}, u32[]{:S(2)}) async-start(bf16[128,176,128]{2,1,0:T(8,128)(2,1)} %fourier.1), calls=%async_computation | async-start | bytes 11534336 | tf_op jit(solution)/shard_map/all_to_all | solution.py:320

commit v2 on v1

--- a/solution.py
+++ b/solution.py
@@ -110,11 +110,10 @@
     return 1.0 - 2.0 * (s * s)
 
 
-def table_kernel(index_ref, owner_ref, main_ref, rest_ref, place_ref, row_ref, spot_ref):
+def table_kernel(slots, index_ref, owner_ref, main_ref, rest_ref, row_ref, spot_ref):
     cols = index_ref.shape[1]
     depth = main_ref.shape[1]
     waves = depth // 2
-    slots = place_ref.shape[0] // LANES
     column = jnp.transpose(jnp.broadcast_to(index_ref[...].astype(F32), (LANES, cols)))[:, :1]
     row = jnp.floor((column + 0.5) * (1.0 / NLON))
     longitude = column - row * NLON
@@ -147,30 +146,28 @@
     first = (lax.broadcasted_iota(jnp.int32, (LANES, cols), 0) * slots).astype(F32)
     spot = jnp.sum(hits_f * (first + earlier), axis=0, keepdims=True).astype(jnp.int32)
     spot_ref[...] = spot
-    place = lax.broadcasted_iota(jnp.int32, (slots * LANES, cols), 0) == spot
-    place_ref[...] = jnp.where(place, 1.0, 0.0).astype(BF16)
 
 
 def tables(index, owner, depth, slots):
     cols = index.shape[1]
     return pl.pallas_call(
-        table_kernel,
+        functools.partial(table_kernel, slots),
         out_shape=(
             jax.ShapeDtypeStruct((cols, depth), BF16),
             jax.ShapeDtypeStruct((cols, depth), BF16),
-            jax.ShapeDtypeStruct((slots * LANES, cols), BF16),
             jax.ShapeDtypeStruct((cols, LANES), F32),
             jax.ShapeDtypeStruct((1, cols), jnp.int32),
         ),
         cost_estimate=pl.CostEstimate(
             flops=60 * cols * depth, bytes_accessed=4 << 20, transcendentals=0
         ),
+        compiler_params=pltpu.CompilerParams(vmem_limit_bytes=24 << 20),
         name="tables",
     )(index, owner)
 
 
 def state_kernel(
-    main_ref, rest_ref, place_ref, row_ref, coeff_ref, out_ref, coeff_s, tail_s, take_s, state_s
+    main_ref, rest_ref, spot_ref, row_ref, coeff_ref, out_ref, coeff_s, tail_s, take_s, state_s
 ):
     v = pl.program_id(0)
     cols = main_ref.shape[0]
@@ -183,44 +180,43 @@
     take_s[...] = block[:, 20:].reshape(sources * 2 * 16, LANES)
     lane = lax.broadcasted_iota(jnp.int32, (1, LANES), 1)
     odd = v % 2
-    tile = v // 2
+    half = pl.ds(pl.multiple_of(v // 2 * LANES, LANES), LANES)
     for u in range(4):
         picked = [take_s[pl.ds(4 * r + u, sources * 2, stride=16), :] for r in range(4)]
         for k in range(GROUP):
             at = (k * 4 + u) * sources * 2
-            kept = tail_s[tile, at : at + sources * 2, :]
+            kept = tail_s[at : at + sources * 2, half]
             for r in range(4):
                 moved = pltpu.roll(picked[r], (64 * odd + 16 * r - REST * k + LANES) % LANES, 1)
                 kept = jnp.where(lane // 16 == 4 * odd + r, moved, kept)
-            tail_s[tile, at : at + sources * 2, :] = kept
+            tail_s[at : at + sources * 2, half] = kept
     row = row_ref[...]
     products = dot(main_ref[...], coeff_s[...])
     main = products[:, :LANES]
     for r in range(1, 4):
         main = jnp.where(row == r, products[:, r * LANES : (r + 1) * LANES], main)
-    state_s[v] = main.astype(BF16)
+    state_s[:, pl.ds(pl.multiple_of(v * LANES, LANES), LANES)] = main.astype(BF16)
 
     @pl.when(v == pl.num_programs(0) - 1)
     def _():
-        place = place_ref[...]
-        tail = jnp.zeros((cols, LANES), F32)
+        products = dot(rest_ref[...], tail_s[...].astype(BF16))
+        folded = []
         for half in range(2):
-            products = dot(rest_ref[...], tail_s[half].astype(BF16))
-            for slot in range(8):
-                u = 2 * half + slot // 4
-                shift = (SLOT_LANES * u - 16 * slot) % LANES
-                moved = products if shift == 0 else pltpu.roll(products, shift, 1)
-                hit = (row == slot % 4) & (lane // SLOT_LANES == u) & (lane % SLOT_LANES < 9)
-                tail = jnp.where(hit, moved, tail)
-        for u in range(4):
-            out_ref[:, u * LANES : (u + 1) * LANES] = dot(place, state_s[u]).astype(BF16)
-        out_ref[:, 4 * LANES :] = dot(place, tail.astype(BF16)).astype(BF16)
-
-
-def column_states(coeff, main_table, rest_table, place, row):
+            part = products[:, half * LANES : (half + 1) * LANES]
+            part = jnp.where((lane // 16 % 4).astype(F32) == row, part, 0.0)
+            part = part + pltpu.roll(part, LANES - 32, 1)
+            folded.append(part + pltpu.roll(part, LANES - 16, 1))
+        tail = jnp.where(lane % 64 < 32, folded[0], pltpu.roll(folded[1], 32, 1))
+        state_s[:, 4 * LANES :] = jnp.where(lane % 32 < 9, tail, 0.0).astype(BF16)
+        place = lax.broadcasted_iota(jnp.int32, (out_ref.shape[0], cols), 0) == spot_ref[...]
+        place = jnp.where(place, 1.0, 0.0).astype(BF16)
+        out_ref[...] = dot(place, state_s[...]).astype(BF16)
+
+
+def column_states(coeff, main_table, rest_table, spot, row, slots):
     sources, rows, _ = coeff.shape
     cols, depth = main_table.shape
-    total = place.shape[0]
+    total = slots * LANES
     whole = lambda x: pl.BlockSpec(x.shape, lambda v: (0,) * x.ndim)
     return pl.pallas_call(
         state_kernel,
@@ -229,19 +225,20 @@
         in_specs=[
             whole(main_table),
             whole(rest_table),
-            whole(place),
+            whole(spot),
             whole(row),
             pl.BlockSpec((sources, rows // 4, LANES), lambda v: (0, v, 0)),
         ],
         out_specs=pl.BlockSpec((total, 5 * LANES), lambda v: (0, 0)),
         scratch_shapes=[
             pltpu.VMEM((depth, 4 * LANES), BF16),
-            pltpu.VMEM((2, depth, LANES), F32),
+            pltpu.VMEM((depth, 2 * LANES), F32),
             pltpu.VMEM((sources * 2 * 16, LANES), F32),
-            pltpu.VMEM((4, cols, LANES), BF16),
+            pltpu.VMEM((cols, 5 * LANES), BF16),
         ],
+        compiler_params=pltpu.CompilerParams(vmem_limit_bytes=28 << 20),
         name="states",
-    )(main_table, rest_table, place, row, coeff)
+    )(main_table, rest_table, spot, row, coeff)
 
 
 def answer_kernel(state_ref, jac_ref, bias_ref, out_ref, jac_s):
@@ -256,7 +253,7 @@
         for v in range(4):
             at = v * levels
             jac_s[v * LANES : (v + 1) * LANES, :] = jac[at : at + LANES].astype(BF16)
-            lo = 4 * LANES + v * SLOT_LANES
+            lo = 4 * LANES + (v % 2 * 2 + v // 2) * SLOT_LANES
             piece = jnp.concatenate(
                 [jac[at + LANES : at + levels], jnp.zeros((16 - rest, channels), F32)], axis=0
             )
@@ -286,6 +283,7 @@
         ],
         out_specs=pl.BlockSpec((total // steps, out_lanes), lambda g: (g, 0)),
         scratch_shapes=[pltpu.VMEM((lanes, channels), BF16)],
+        compiler_params=pltpu.CompilerParams(vmem_limit_bytes=20 << 20),
         name="answers",
     )(states, jac_t, bias)
 
@@ -298,10 +296,9 @@
     place = jnp.where(place, 1.0, 0.0).astype(BF16)
     channels = depart_ref.shape[0]
     width = grad_ref.shape[0]
-    depart = jnp.transpose(dot(place, back_ref[:, : 3 * LANES]))
-    depart_ref[...] = depart[:channels].astype(BF16)
-    grad = jnp.transpose(dot(place, back_ref[:, 3 * LANES :]))
-    grad_ref[...] = grad[:width].astype(BF16)
+    both = jnp.transpose(dot(place, back_ref[...]))
+    depart_ref[...] = both[:channels].astype(BF16)
+    grad_ref[...] = both[3 * LANES : 3 * LANES + width].astype(BF16)
 
 
 def collect(spot, back, channels, width):
@@ -312,6 +309,7 @@
             jax.ShapeDtypeStruct((channels, cols), BF16),
             jax.ShapeDtypeStruct((width, cols), BF16),
         ),
+        compiler_params=pltpu.CompilerParams(vmem_limit_bytes=20 << 20),
         name="collect",
     )(spot, back)
 
@@ -329,11 +327,11 @@
     var = lax.axis_index("lat") // 2
     pair_base = (lax.axis_index("wave") * pairs).astype(jnp.int32).reshape(1)
     blocks = fourier_blocks(control, spread[var], vertical[var], legendre, pair_base, device_count)
-    main_table, rest_table, place, row, spot = tables(
+    main_table, rest_table, row, spot = tables(
         column_index.reshape(1, cols), column_owner.reshape(1, cols), 4 * pairs * wave_count, slots
     )
     coeff = exchange(blocks).reshape(wave_count, -1, LANES)
-    outgoing = column_states(coeff, main_table, rest_table, place, row)
+    outgoing = column_states(coeff, main_table, rest_table, spot, row, slots)
     lanes = outgoing.shape[1]
     states = exchange(outgoing.reshape(device_count, slots, lanes))
     jac_t = jnp.transpose(jacobian[0])

time: 187 us -> 179 us (0.957)
  Pallas kernels: 42 us -> 32.3 us
  local copies, waits for them, and re-layouts: 4.16 us -> 6.58 us
  blocking collectives: 65.8 us -> 63.9 us
    pallas_call x1, Pallas kernels: 10.5 us -> 7.54 us  [column_states(): pl.pallas_call(state_kernel, out_shape=jax.ShapeDtypeStruct((total, 5 * L...]
    pallas_call x1, Pallas kernels: 7.87 us -> 5.15 us  [tables(): pl.pallas_call(functools.partial(table_kernel, slots), out_shape=(jax.Sha...]
    unnamed x4 -> x16, local copies, waits for them, and re-layouts: 2.1 us -> 4.53 us
    pallas_call x1, Pallas kernels: 4.82 us -> 2.59 us  [answers(): pl.pallas_call(answer_kernel, out_shape=jax.ShapeDtypeStruct((total, out_...]
  transfers between devices with their start and end apart: 1 -> 1, of which waited for: 1 -> 1; matrix products, arithmetic and copies ran while one was open for 0% -> 0% of each run, Pallas kernels for 4% -> 3%
where the time goes in v2:
time: 179 us
  blocking collectives  63.9 us (36%)
  waiting for transfers between devices  63.3 us (35%)
  Pallas kernels  32.3 us (18%)
  starting transfers between devices  11.9 us (7%)
  local copies, waits for them, and re-layouts  6.58 us (4%)
    all_to_all x2, blocking collectives, exchange(): lax.all_to_all(x, ('wave', 'lat'), split_axis=0, concat_axis=0, tiled=True)  63.9 us
    all_to_all x1, waiting for transfers between devices, exchange(): lax.all_to_all(x, ('wave', 'lat'), split_axis=0, concat_axis=0, tiled=True)  63.3 us
    pallas_call x1, Pallas kernels, fourier_blocks(): pl.pallas_call(fourier_kernel, out_shape=jax.ShapeDtypeStruct((dests, 32...  14.5 us
    all_to_all x1, starting transfers between devices, exchange(): lax.all_to_all(x, ('wave', 'lat'), split_axis=0, concat_axis=0, tiled=True)  11.9 us
    pallas_call x1, Pallas kernels, column_states(): pl.pallas_call(state_kernel, out_shape=jax.ShapeDtypeStruct((total, 5 * L...  7.54 us
    pallas_call x1, Pallas kernels, tables(): pl.pallas_call(functools.partial(table_kernel, slots), out_shape=(jax.Sha...  5.15 us
    unnamed x16, local copies, waits for them, and re-layouts  4.53 us
  transfers between devices with their start and end apart: 1, of which 1 were waited for; matrix products, arithmetic and copies ran while one was open for 0% of the time, Pallas kernels for 3%

profile of v2, /device:TPU:1, one launch (start us, length us, event | category | flops | bytes accessed | tf_op | source)
XLA Modules:
  0.0 178.7 jit_solution(16014614778391636951)
XLA Ops:
  0.6 0.0 copy-start
  0.7 1.3 copy-done
  2.0 0.3 constant_dynamic-slice_fusion.1
  2.3 0.8 copy.16
  3.1 1.1 constant_dynamic-slice_fusion
  4.2 0.6 pad.4.vert_ref
  4.8 14.5 %fourier.1 = bf16[128,176,128]{2,1,0:T(8,128)(2,1)} custom-call(s32[1]{0:T(128)} %bitcast.2.base_ref, bf16[20,1,137,641]{3,2,1,0:T(8,128)(2,1)} %bitcast.29, f32[137,640]{1,0:T(8,128)} %bitcast.30, bf16[144,137]{1,0:T(8,128)(2,1)} %pad.4.vert_ref, bf16[20,641,512]{2,1,0:T(8,128)(2,1)} %leg_ref.1), custom_call_target="tpu_custom_call" | custom-call | tf_op jit(solution)/shard_map/fourier/pallas_call | solution.py:86
  19.4 0.0 copy-start.5
  19.4 0.0 copy-start.6
  19.4 11.9 %all-to-all-start = ((bf16[128,176,128]{2,1,0:T(8,128)(2,1)}), bf16[128,176,128]{2,1,0:T(8,128)(2,1)}, u32[]{:S(2)}, u32[]{:S(2)}) async-start(bf16[128,176,128]{2,1,0:T(8,128)(2,1)} %fourier.1), calls=%async_computation | async-start | bytes 11534336 | tf_op jit(solution)/shard_map/all_to_all | solution.py:318
  31.2 0.0 copy-done.5
  31.3 0.0 copy-done.6
  31.3 5.1 %tables.1 = (bf16[512,1280]{1,0:T(8,128)(2,1)S(1)}, bf16[512,1280]{1,0:T(8,128)(2,1)S(1)}, f32[512,128]{1,0:T(8,128)S(1)}, s32[1,512]{1,0:T(1,128)S(1)}) custom-call(s32[1,512]{1,0:T(1,128)S(1)} %bitcast.27, s32[1,512]{1,0:T(1,128)S(1)} %bitcast.28), custom_call_target="tpu_custom_call" | custom-call | flops 39321600 | bytes 4194304 | tf_op jit(solution)/shard_map/tables/pallas_call | solution.py:153
  36.4 0.0 copy-start.1
  36.4 1.1 copy-done.1
  37.5 63.3 %all-to-all-done = bf16[128,176,128]{2,1,0:T(8,128)(2,1)} async-done(((bf16[128,176,128]{2,1,0:T(8,128)(2,1)}), bf16[128,176,128]{2,1,0:T(8,128)(2,1)}, u32[]{:S(2)}, u32[]{:S(2)}) %all-to-all-start) | async-done | bytes 5767200 | tf_op jit(solution)/shard_map/all_to_all | solution.py:318
  100.8 0.0 copy-start.2
  100.8 1.3 copy-done.2
  102.1 7.5 %states.1 = bf16[1024,640]{1,0:T(8,128)(2,1)S(1)} custom-call(bf16[512,1280]{1,0:T(8,128)(2,1)S(1)} %get-tuple-element.9.main_ref, bf16[512,1280]{1,0:T(8,128)(2,1)S(1)} %copy-done.2, s32[1,512]{1,0:T(1,128)S(1)} %get-tuple-element.8.spot_ref, f32[512,128]{1,0:T(8,128)S(1)} %get-tuple-element.11.row_ref, bf16[16,1408,128]{2,1,0:T(8,128)(2,1)} %bitcast.7.coeff_ref), custom_call_target="tpu_custom_call" | custom-call | tf_op jit(solution)/shard_map/states/pallas_call | solution.py:221
  109.7 0.0 copy-start.3
  109.7 0.0 copy-start.4
  109.7 29.2 %all_to_all.15 = bf16[128,8,640]{2,1,0:T(8,128)(2,1)S(1)} all-to-all(bf16[128,8,640]{2,1,0:T(8,128)(2,1)S(1)} %bitcast.25), channel_id=1, replica_groups=mesh['wave'=16,'lat'=8] {'wave','lat'}, dimensions={0} | all-to-all | bytes 2621440 | tf_op jit(solution)/shard_map/all_to_all | solution.py:318
  138.9 0.0 copy-done.3
  138.9 0.0 copy-done.4
  138.9 2.6 %answers.1 = bf16[1024,1024]{1,0:T(8,128)(2,1)S(1)} custom-call(bf16[1024,640]{1,0:T(8,128)(2,1)S(1)} %bitcast.24, bf16[548,366]{1,0:T(8,128)(2,1)S(1)} %bitcast.26, f32[1,366]{1,0:T(1,128)S(1)} %copy-done.4), custom_call_target="tpu_custom_call" | custom-call | tf_op jit(solution)/shard_map/answers/pallas_call | solution.py:275
  141.5 34.7 %all_to_all.16 = bf16[128,8,1024]{2,1,0:T(8,128)(2,1)S(1)} all-to-all(bf16[128,8,1024]{2,1,0:T(8,128)(2,1)S(1)} %bitcast.22), channel_id=1, replica_groups=mesh['wave'=16,'lat'=8] {'wave','lat'}, dimensions={0} | all-to-all | bytes 4194304 | tf_op jit(solution)/shard_map/all_to_all | solution.py:318
  176.2 2.5 %collect.1 = (bf16[366,512]{1,0:T(8,128)(2,1)}, bf16[548,512]{1,0:T(8,128)(2,1)}) custom-call(s32[1,512]{1,0:T(1,128)S(1)} %get-tuple-element.8.spot_ref, bf16[1024,1024]{1,0:T(8,128)(2,1)S(1)} %bitcast.23), custom_call_target="tpu_custom_call" | custom-call | tf_op jit(solution)/shard_map/collect/pallas_call | solution.py:306
  (1 shorter events, 0.0 us)
Async XLA Ops:
  0.6 1.4 copy-start
  19.4 11.9 %copy-start.5 = (s32[512]{0:T(512)S(1)}, s32[512]{0:T(512)}, u32[]{:S(2)}) copy-start(s32[512]{0:T(512)} %param.12) | copy-start | bytes 6148
  19.4 11.9 %copy-start.6 = (s32[512,1]{0,1:T(1,128)S(1)}, s32[512,1]{0,1:T(1,128)}, u32[]{:S(2)}) copy-start(s32[512,1]{0,1:T(1,128)} %param.13) | copy-start | bytes 6148
  19.4 81.5 %all-to-all-start = ((bf16[128,176,128]{2,1,0:T(8,128)(2,1)}), bf16[128,176,128]{2,1,0:T(8,128)(2,1)}, u32[]{:S(2)}, u32[]{:S(2)}) async-start(bf16[128,176,128]{2,1,0:T(8,128)(2,1)} %fourier.1), calls=%async_computation | async-start | bytes 11534336 | tf_op jit(solution)/shard_map/all_to_all | solution.py:318
  36.4 1.1 copy-start.1
  100.8 1.3 copy-start.2
  109.7 29.2 %copy-start.3 = (bf16[1,366,548]{1,2,0:T(8,128)(2,1)S(1)}, bf16[1,366,548]{1,2,0:T(8,128)(2,1)}, u32[]{:S(2)}) copy-start(bf16[1,366,548]{1,2,0:T(8,128)(2,1)} %param.14) | copy-start | bytes 1203412
  109.7 29.2 %copy-start.4 = (f32[1,366]{1,0:T(1,128)S(1)}, f32[1,366]{1,0:T(1,128)}, u32[]{:S(2)}) copy-start(f32[1,366]{1,0:T(1,128)} %bias_ref.1) | copy-start | bytes 4396

commit v3 on v2

--- a/solution.py
+++ b/solution.py
@@ -21,57 +21,123 @@
     return jnp.dot(a, b, preferred_element_type=F32)
 
 
-def fourier_kernel(base_ref, ctrl_ref, spread_ref, vert_ref, leg_ref, out_ref, main_s, rem_s):
+def fourier_kernel(
+    base_ref,
+    ctrl_ref,
+    spread_ref,
+    vert_ref,
+    leg_ref,
+    out_ref,
+    main_s,
+    rest_s,
+    rem_s,
+    spread_s,
+    second_s,
+    first_s,
+    scaled_s,
+    spec_s,
+    vert_s,
+):
     slots = ctrl_ref.shape[3]
     waves = slots - 1
+    modes = ctrl_ref.shape[2]
     rows = leg_ref.shape[2]
     dests = out_ref.shape[0]
-    steps = pl.num_programs(0) - 1
-    g = pl.program_id(0)
-
-    @pl.when(g == 0)
+    steps = pl.num_programs(0) - 3
+    t = pl.program_id(0)
+    lane = lax.broadcasted_iota(jnp.int32, (1, LANES), 1)
+    slot = lax.broadcasted_iota(jnp.int32, (1, slots), 1)
+
+    def align(step):
+        pair = base_ref[0] + step * 4
+        skip = pair // LANES
+        shift = pair - skip * LANES
+        last = None
+        for k in range(6):
+            if last is None:
+                last = pltpu.roll(
+                    spread_s[:, pl.ds(pl.multiple_of(skip * LANES, LANES), LANES)], LANES - shift, 1
+                )
+            after = spread_s[:, pl.ds(pl.multiple_of((skip + k + 1) * LANES, LANES), LANES)]
+            after = pltpu.roll(after, LANES - shift, 1)
+            first_s[:, k * LANES : (k + 1) * LANES] = jnp.where(lane < LANES - shift, last, after)
+            last = after
+
+    def scale(step, i):
+        pair = base_ref[0] + step * 4 + i
+        last = first_s[:, :LANES]
+        last = pltpu.roll(last, LANES - i, 1) if i else last
+        for k in range(5):
+            at = slice(k * LANES, (k + 1) * LANES)
+            after = first_s[:, (k + 1) * LANES : (k + 2) * LANES]
+            after = pltpu.roll(after, LANES - i, 1) if i else after
+            factor = jnp.where(lane < LANES - i, last, after) if i else last
+            last = after
+            if k >= 2:
+                factor = jnp.where(lane + k * LANES < waves - pair, factor, second_s[:, at])
+            scaled_s[:, at] = (ctrl_ref[i, 0, :, at].astype(F32) * factor).astype(BF16)
+        end = ctrl_ref[i, 0, :, waves:].astype(F32) * second_s[:, waves : waves + 1]
+        scaled_s[:, waves : waves + 1] = end.astype(BF16)
+        spec_s[i] = dot(vert_s[...], scaled_s[:, :slots]).astype(BF16)
+
+    def sums(step, i, early):
+        pair = base_ref[0] + step * 4 + i
+        spec = spec_s[i]
+        lo, hi = (512, slots) if early else (256, 512)
+        mixed = spec[:, lo:hi]
+        keep = slot[:, lo:hi] < waves - pair
+        zero = jnp.zeros_like(mixed)
+        both = jnp.concatenate(
+            [jnp.where(keep, mixed, zero), jnp.where(keep, zero, mixed)], axis=0
+        )
+        both = dot(both, leg_ref[i, lo:hi, :])
+        half_rows = spec.shape[0]
+        first = both[:half_rows] + dot(spec[:, :lo], leg_ref[i, :lo, :])
+        second = both[half_rows:]
+        if not early:
+            second = second + dot(spec[:, hi:], leg_ref[i, hi:, :])
+        parts = (first, second)
+        for h in range(2):
+            j = 2 * i + h
+            main_s[pl.ds(j, rows, stride=8), :] = jnp.transpose(parts[h][:LANES])
+            rest_s[step, 16 * j : 16 * j + 16, :] = parts[h][LANES:]
+
+    def emit():
+        out_ref[...] = main_s[...].reshape(dests, 32, LANES).astype(BF16)
+
+    @pl.when(t == 0)
     def _():
+        spread_s[:, waves:] = jnp.zeros((modes, spread_s.shape[1] - waves), F32)
+        spread_s[:, :waves] = spread_ref[...]
+        second_s[:, :waves] = pltpu.roll(spread_ref[...], 1, 1)
+        second_s[:, waves : waves + 1] = spread_ref[:, waves - 1 :]
+        vert_s[...] = jnp.zeros_like(vert_s)
+        vert_s[:modes, :] = vert_ref[...]
         rem_s[...] = jnp.zeros_like(rem_s)
-
-    @pl.when(g < steps)
+        align(0)
+        for i in range(4):
+            scale(0, i)
+
+    for early in (True, False):
+
+        @pl.when((t > 0) & (t <= steps) & ((base_ref[0] + 4 * t <= 128) == early))
+        def _():
+            emit()
+            align(jnp.minimum(t, steps - 1))
+            for i in range(4):
+                sums(t - 1, i, early)
+                scale(jnp.minimum(t, steps - 1), i)
+
+    @pl.when(t == steps + 1)
     def _():
-        spread = spread_ref[...]
-        lane = lax.broadcasted_iota(jnp.int32, (1, waves), 1)
-        slot = lax.broadcasted_iota(jnp.int32, (1, slots), 1)
-        second_scale = pltpu.roll(spread, 1, 1)
-        pair0 = base_ref[0] + g * 4
-        rests = []
-        for i in range(4):
-            pair = pair0 + i
-            first_scale = pltpu.roll(spread, waves - pair, 1)
-            scale = jnp.where(lane < waves - pair, first_scale, second_scale)
-            scale = jnp.concatenate([scale, spread[:, waves - 1 :]], axis=1)
-            scaled = (ctrl_ref[i, 0].astype(F32) * scale).astype(BF16)
-            spec = dot(vert_ref[...], scaled).astype(BF16)
-            keep = slot < waves - pair
-            zero = jnp.zeros_like(spec)
-            first = jnp.where(keep, spec, zero)
-            second = jnp.where(keep, zero, spec)
-            both = jnp.concatenate([first[:, 256:], second[:, 256:]], axis=0)
-            sums = dot(both, leg_ref[i, 256:, :])
-            half_rows = spec.shape[0]
-            parts = (sums[:half_rows] + dot(first[:, :256], leg_ref[i, :256, :]), sums[half_rows:])
-            for h in range(2):
-                j = 2 * i + h
-                main_s[pl.ds(j, rows, stride=8), :] = jnp.transpose(parts[h][:LANES])
-                rests.append(parts[h][LANES : LANES + REST])
-        out_ref[...] = main_s[...].reshape(dests, 32, LANES).astype(BF16)
-        for step in range(5):
-
-            @pl.when(g == step)
-            def _():
-                for j in range(8):
-                    k = 8 * step + j
-                    at = LANES * (k // GROUP) + REST * (k % GROUP)
-                    rem_s[at : at + REST, :] = rests[j]
-
-    @pl.when(g == steps)
+        emit()
+
+    @pl.when(t == steps + 2)
     def _():
+        for k in range(8 * steps):
+            at = LANES * (k // GROUP) + REST * (k % GROUP)
+            lo = 16 * (k % 8)
+            rem_s[at : at + REST, :] = rest_s[k // 8, lo : lo + REST, :]
         for u in range(4):
             main_s[pl.ds(u, rows, stride=4), :] = jnp.transpose(rem_s[u * LANES : (u + 1) * LANES])
         out_ref[:, :16, :] = main_s[: 4 * rows, :].reshape(dests, 16, LANES).astype(BF16)
@@ -81,23 +147,32 @@
     pairs, slots, _, modes = control.shape
     rows = legendre.shape[2]
     ctrl = jnp.transpose(control, (0, 2, 3, 1))
-    vert = jnp.pad(vertical, ((0, 144 - vertical.shape[0]), (0, 0)))
     steps = pairs // 4
     return pl.pallas_call(
         fourier_kernel,
         out_shape=jax.ShapeDtypeStruct((dests, 32 * steps + 16, LANES), BF16),
-        grid=(steps + 1,),
+        grid=(steps + 3,),
         in_specs=[
             pl.BlockSpec(memory_space=pltpu.SMEM),
-            pl.BlockSpec((4, 1, modes, slots), lambda g: (jnp.minimum(g, steps - 1), 0, 0, 0)),
-            pl.BlockSpec((modes, slots - 1), lambda g: (0, 0)),
-            pl.BlockSpec((144, modes), lambda g: (0, 0)),
-            pl.BlockSpec((4, slots, rows), lambda g: (jnp.minimum(g, steps - 1), 0, 0)),
+            pl.BlockSpec((4, 1, modes, slots), lambda t: (jnp.minimum(t, steps - 1), 0, 0, 0)),
+            pl.BlockSpec((modes, slots - 1), lambda t: (0, 0)),
+            pl.BlockSpec((modes, modes), lambda t: (0, 0)),
+            pl.BlockSpec((4, slots, rows), lambda t: (jnp.clip(t - 1, 0, steps - 1), 0, 0)),
         ],
-        out_specs=pl.BlockSpec((dests, 32, LANES), lambda g: (0, g, 0)),
-        scratch_shapes=[pltpu.VMEM((rows * 8, LANES), F32), pltpu.VMEM((4 * LANES, rows), F32)],
+        out_specs=pl.BlockSpec((dests, 32, LANES), lambda t: (0, jnp.maximum(t - 2, 0), 0)),
+        scratch_shapes=[
+            pltpu.VMEM((rows * 8, LANES), F32),
+            pltpu.VMEM((steps, LANES, rows), F32),
+            pltpu.VMEM((4 * LANES, rows), F32),
+            pltpu.VMEM((modes, 9 * LANES), F32),
+            pltpu.VMEM((modes, 6 * LANES), F32),
+            pltpu.VMEM((modes, 6 * LANES), F32),
+            pltpu.VMEM((modes, 6 * LANES), BF16),
+            pltpu.VMEM((4, 144, slots), BF16),
+            pltpu.VMEM((144, modes), BF16),
+        ],
         name="fourier",
-    )(pair_base, ctrl, jnp.transpose(spread), vert, legendre)
+    )(pair_base, ctrl, jnp.transpose(spread), vertical, legendre)
 
 
 def cosine(turns):
@@ -110,31 +185,30 @@
     return 1.0 - 2.0 * (s * s)
 
 
-def table_kernel(slots, index_ref, owner_ref, main_ref, rest_ref, row_ref, spot_ref):
+def table_kernel(slots, index_ref, owner_ref, main_ref, row_ref, spot_ref):
     cols = index_ref.shape[1]
     depth = main_ref.shape[1]
     waves = depth // 2
-    column = jnp.transpose(jnp.broadcast_to(index_ref[...].astype(F32), (LANES, cols)))[:, :1]
+    column = jnp.transpose(jnp.broadcast_to(index_ref[...].astype(F32), (LANES, cols)))
     row = jnp.floor((column + 0.5) * (1.0 / NLON))
+    row_ref[...] = row
+    column = column[:, :1]
+    row = row[:, :1]
     longitude = column - row * NLON
-    row_ref[...] = jnp.broadcast_to(row, row_ref.shape)
     lane = lax.broadcasted_iota(jnp.int32, (1, depth), 1)
 
-    def fill(ref, source, part, local):
-        pair = source * 20 + local // 2
-        wave = jnp.where(local % 2 == 0, pair, waves - 1 - pair)
-        weight = jnp.where(wave == 0, 1.0, 2.0).astype(F32)
-        wave_f = wave.astype(F32)
-        shift = part.astype(F32) * (NLON // 4)
-        for c in range(0, cols, 64):
-            turns = longitude[c : c + 64] * wave_f + shift
-            turns = turns - jnp.floor(turns * (1.0 / NLON) + 0.5) * NLON
-            ref[c : c + 64, :] = (weight * cosine(turns * (1.0 / NLON))).astype(BF16)
-
-    inner = lane % 80
-    fill(main_ref, lane // 80, inner // 40, inner % 40)
-    inner = lane % 128
-    fill(rest_ref, inner % 32 // 2, inner % 2, inner // 32 * GROUP + lane // 128)
+    source = lane // 80
+    part = lane % 80 // 40
+    local = lane % 40
+    pair = source * 20 + local // 2
+    wave = jnp.where(local % 2 == 0, pair, waves - 1 - pair)
+    weight = jnp.where(wave == 0, 1.0, 2.0).astype(F32)
+    wave_f = wave.astype(F32)
+    shift = part.astype(F32) * (NLON // 4)
+    for c in range(0, cols, 64):
+        turns = longitude[c : c + 64] * wave_f + shift
+        turns = turns - jnp.floor(turns * (1.0 / NLON) + 0.5) * NLON
+        main_ref[c : c + 64, :] = (weight * cosine(turns * (1.0 / NLON))).astype(BF16)
 
     hits = lax.broadcasted_iota(jnp.int32, (LANES, cols), 0) == owner_ref[...]
     hits_f = jnp.where(hits, 1.0, 0.0).astype(F32)
@@ -154,7 +228,6 @@
         functools.partial(table_kernel, slots),
         out_shape=(
             jax.ShapeDtypeStruct((cols, depth), BF16),
-            jax.ShapeDtypeStruct((cols, depth), BF16),
             jax.ShapeDtypeStruct((cols, LANES), F32),
             jax.ShapeDtypeStruct((1, cols), jnp.int32),
         ),
@@ -167,7 +240,7 @@
 
 
 def state_kernel(
-    main_ref, rest_ref, spot_ref, row_ref, coeff_ref, out_ref, coeff_s, tail_s, take_s, state_s
+    main_ref, spot_ref, row_ref, coeff_ref, out_ref, coeff_s, tail_s, take_s, state_s
 ):
     v = pl.program_id(0)
     cols = main_ref.shape[0]
@@ -180,16 +253,15 @@
     take_s[...] = block[:, 20:].reshape(sources * 2 * 16, LANES)
     lane = lax.broadcasted_iota(jnp.int32, (1, LANES), 1)
     odd = v % 2
-    half = pl.ds(pl.multiple_of(v // 2 * LANES, LANES), LANES)
     for u in range(4):
         picked = [take_s[pl.ds(4 * r + u, sources * 2, stride=16), :] for r in range(4)]
         for k in range(GROUP):
-            at = (k * 4 + u) * sources * 2
-            kept = tail_s[at : at + sources * 2, half]
+            at = pl.ds(v // 2 * depth + u * GROUP + k, sources * 2, stride=4 * GROUP)
+            kept = tail_s[at, :]
             for r in range(4):
                 moved = pltpu.roll(picked[r], (64 * odd + 16 * r - REST * k + LANES) % LANES, 1)
                 kept = jnp.where(lane // 16 == 4 * odd + r, moved, kept)
-            tail_s[at : at + sources * 2, half] = kept
+            tail_s[at, :] = kept
     row = row_ref[...]
     products = dot(main_ref[...], coeff_s[...])
     main = products[:, :LANES]
@@ -199,7 +271,8 @@
 
     @pl.when(v == pl.num_programs(0) - 1)
     def _():
-        products = dot(rest_ref[...], tail_s[...].astype(BF16))
+        wide = jnp.concatenate([tail_s[:depth], tail_s[depth:]], axis=1)
+        products = dot(main_ref[...], wide.astype(BF16))
         folded = []
         for half in range(2):
             part = products[:, half * LANES : (half + 1) * LANES]
@@ -213,7 +286,7 @@
         out_ref[...] = dot(place, state_s[...]).astype(BF16)
 
 
-def column_states(coeff, main_table, rest_table, spot, row, slots):
+def column_states(coeff, main_table, spot, row, slots):
     sources, rows, _ = coeff.shape
     cols, depth = main_table.shape
     total = slots * LANES
@@ -224,7 +297,6 @@
         grid=(4,),
         in_specs=[
             whole(main_table),
-            whole(rest_table),
             whole(spot),
             whole(row),
             pl.BlockSpec((sources, rows // 4, LANES), lambda v: (0, v, 0)),
@@ -232,13 +304,13 @@
         out_specs=pl.BlockSpec((total, 5 * LANES), lambda v: (0, 0)),
         scratch_shapes=[
             pltpu.VMEM((depth, 4 * LANES), BF16),
-            pltpu.VMEM((depth, 2 * LANES), F32),
+            pltpu.VMEM((2 * depth, LANES), F32),
             pltpu.VMEM((sources * 2 * 16, LANES), F32),
             pltpu.VMEM((cols, 5 * LANES), BF16),
         ],
         compiler_params=pltpu.CompilerParams(vmem_limit_bytes=28 << 20),
         name="states",
-    )(main_table, rest_table, spot, row, coeff)
+    )(main_table, spot, row, coeff)
 
 
 def answer_kernel(state_ref, jac_ref, bias_ref, out_ref, jac_s):
@@ -327,11 +399,12 @@
     var = lax.axis_index("lat") // 2
     pair_base = (lax.axis_index("wave") * pairs).astype(jnp.int32).reshape(1)
     blocks = fourier_blocks(control, spread[var], vertical[var], legendre, pair_base, device_count)
-    main_table, rest_table, row, spot = tables(
-        column_index.reshape(1, cols), column_owner.reshape(1, cols), 4 * pairs * wave_count, slots
+    index = column_index.reshape(1, cols)
+    main_table, row, spot = tables(
+        index, column_owner.reshape(1, cols), 4 * pairs * wave_count, slots
     )
     coeff = exchange(blocks).reshape(wave_count, -1, LANES)
-    outgoing = column_states(coeff, main_table, rest_table, spot, row, slots)
+    outgoing = column_states(coeff, main_table, spot, row, slots)
     lanes = outgoing.shape[1]
     states = exchange(outgoing.reshape(device_count, slots, lanes))
     jac_t = jnp.transpose(jacobian[0])

time: 179 us -> 178 us (level)
  waiting for transfers between devices: 63.3 us -> 66.9 us
  Pallas kernels: 32.3 us -> 29.8 us
  local copies, waits for them, and re-layouts: 6.58 us -> 4.16 us
    all_to_all x1, waiting for transfers between devices: 63.3 us -> 66.9 us  [exchange(): lax.all_to_all(x, ('wave', 'lat'), split_axis=0, concat_axis=0, tiled=True)]
    pallas_call x1, Pallas kernels: 5.15 us -> 2.69 us  [tables(): pl.pallas_call(functools.partial(table_kernel, slots), out_shape=(jax.Sha...]
    unnamed x16 -> x12, local copies, waits for them, and re-layouts: 4.53 us -> 2.76 us
  transfers between devices with their start and end apart: 1 -> 1, of which waited for: 1 -> 1; matrix products, arithmetic and copies ran while one was open for 0% -> 0% of each run, Pallas kernels for 3% -> 2%
where the time goes in v3:
time: 178 us; the launch traced here: 177 us
  waiting for transfers between devices  66.9 us (38%)
  blocking collectives  63.9 us (36%)
  Pallas kernels  29.8 us (17%)
  starting transfers between devices  11.8 us (7%)
  local copies, waits for them, and re-layouts  4.16 us (2%)
    all_to_all x1, waiting for transfers between devices, exchange(): lax.all_to_all(x, ('wave', 'lat'), split_axis=0, concat_axis=0, tiled=True)  66.9 us
    all_to_all x2, blocking collectives, exchange(): lax.all_to_all(x, ('wave', 'lat'), split_axis=0, concat_axis=0, tiled=True)  63.9 us
    pallas_call x1, Pallas kernels, fourier_blocks(): pl.pallas_call(fourier_kernel, out_shape=jax.ShapeDtypeStruct((dests, 32...  14.4 us
    all_to_all x1, starting transfers between devices, exchange(): lax.all_to_all(x, ('wave', 'lat'), split_axis=0, concat_axis=0, tiled=True)  11.8 us
    pallas_call x1, Pallas kernels, column_states(): pl.pallas_call(state_kernel, out_shape=jax.ShapeDtypeStruct((total, 5 * L...  7.62 us
  transfers between devices with their start and end apart: 1, of which 1 were waited for; matrix products, arithmetic and copies ran while one was open for 0% of the time, Pallas kernels for 2%

profile of v3, /device:TPU:1, one launch (start us, length us, event | category | flops | bytes accessed | tf_op | source)
XLA Modules:
  0.0 177.3 jit_solution(3195721410051530186)
XLA Ops:
  0.6 0.0 copy-start
  0.7 1.3 copy-done
  2.0 0.3 constant_dynamic-slice_fusion.1
  2.3 0.8 copy.16
  3.1 1.1 constant_dynamic-slice_fusion
  4.2 0.6 copy.17
  4.8 14.4 %fourier.1 = bf16[128,176,128]{2,1,0:T(8,128)(2,1)} custom-call(s32[1]{0:T(128)} %bitcast.2.base_ref, bf16[20,1,137,641]{3,2,1,0:T(8,128)(2,1)} %bitcast.29, f32[137,640]{1,0:T(8,128)} %bitcast.30, bf16[137,137]{1,0:T(8,128)(2,1)} %bitcast.31, bf16[20,641,512]{2,1,0:T(8,128)(2,1)} %leg_ref.1), custom_call_target="tpu_custom_call" | custom-call | tf_op jit(solution)/shard_map/fourier/pallas_call | solution.py:151
  19.2 0.0 copy-start.3
  19.2 0.0 copy-start.4
  19.2 11.8 %all-to-all-start = ((bf16[128,176,128]{2,1,0:T(8,128)(2,1)}), bf16[128,176,128]{2,1,0:T(8,128)(2,1)}, u32[]{:S(2)}, u32[]{:S(2)}) async-start(bf16[128,176,128]{2,1,0:T(8,128)(2,1)} %fourier.1), calls=%async_computation | async-start | bytes 11534336 | tf_op jit(solution)/shard_map/all_to_all | solution.py:390
  31.0 0.0 copy-done.3
  31.0 0.0 copy-done.4
  31.0 2.7 %tables.1 = (bf16[512,1280]{1,0:T(8,128)(2,1)S(1)}, f32[512,128]{1,0:T(8,128)S(1)}, s32[1,512]{1,0:T(1,128)S(1)}) custom-call(s32[1,512]{1,0:T(1,128)S(1)} %bitcast.27, s32[1,512]{1,0:T(1,128)S(1)} %bitcast.28), custom_call_target="tpu_custom_call" | custom-call | flops 39321600 | bytes 4194304 | tf_op jit(solution)/shard_map/tables/pallas_call | solution.py:227
  33.7 66.9 %all-to-all-done = bf16[128,176,128]{2,1,0:T(8,128)(2,1)} async-done(((bf16[128,176,128]{2,1,0:T(8,128)(2,1)}), bf16[128,176,128]{2,1,0:T(8,128)(2,1)}, u32[]{:S(2)}, u32[]{:S(2)}) %all-to-all-start) | async-done | bytes 5767200 | tf_op jit(solution)/shard_map/all_to_all | solution.py:390
  100.6 7.6 %states.1 = bf16[1024,640]{1,0:T(8,128)(2,1)S(1)} custom-call(bf16[512,1280]{1,0:T(8,128)(2,1)S(1)} %get-tuple-element.8.main_ref, s32[1,512]{1,0:T(1,128)S(1)} %get-tuple-element.7.spot_ref, f32[512,128]{1,0:T(8,128)S(1)} %get-tuple-element.9.row_ref, bf16[16,1408,128]{2,1,0:T(8,128)(2,1)} %bitcast.7.coeff_ref), custom_call_target="tpu_custom_call" | custom-call | tf_op jit(solution)/shard_map/states/pallas_call | solution.py:294
  108.2 0.0 copy-start.1
  108.2 0.0 copy-start.2
  108.2 29.2 %all_to_all.15 = bf16[128,8,640]{2,1,0:T(8,128)(2,1)S(1)} all-to-all(bf16[128,8,640]{2,1,0:T(8,128)(2,1)S(1)} %bitcast.24), channel_id=1, replica_groups=mesh['wave'=16,'lat'=8] {'wave','lat'}, dimensions={0} | all-to-all | bytes 2621440 | tf_op jit(solution)/shard_map/all_to_all | solution.py:390
  137.4 0.0 copy-done.1
  137.4 0.0 copy-done.2
  137.4 2.6 %answers.1 = bf16[1024,1024]{1,0:T(8,128)(2,1)S(1)} custom-call(bf16[1024,640]{1,0:T(8,128)(2,1)S(1)} %bitcast.25, bf16[548,366]{1,0:T(8,128)(2,1)S(1)} %bitcast.26, f32[1,366]{1,0:T(1,128)S(1)} %copy-done.2), custom_call_target="tpu_custom_call" | custom-call | tf_op jit(solution)/shard_map/answers/pallas_call | solution.py:347
  140.0 34.7 %all_to_all.16 = bf16[128,8,1024]{2,1,0:T(8,128)(2,1)S(1)} all-to-all(bf16[128,8,1024]{2,1,0:T(8,128)(2,1)S(1)} %bitcast.22), channel_id=1, replica_groups=mesh['wave'=16,'lat'=8] {'wave','lat'}, dimensions={0} | all-to-all | bytes 4194304 | tf_op jit(solution)/shard_map/all_to_all | solution.py:390
  174.8 2.5 %collect.1 = (bf16[366,512]{1,0:T(8,128)(2,1)}, bf16[548,512]{1,0:T(8,128)(2,1)}) custom-call(s32[1,512]{1,0:T(1,128)S(1)} %get-tuple-element.7.spot_ref, bf16[1024,1024]{1,0:T(8,128)(2,1)S(1)} %bitcast.23), custom_call_target="tpu_custom_call" | custom-call | tf_op jit(solution)/shard_map/collect/pallas_call | solution.py:378
Async XLA Ops:
  0.6 1.4 copy-start
  19.2 11.8 %copy-start.3 = (s32[512]{0:T(512)S(1)}, s32[512]{0:T(512)}, u32[]{:S(2)}) copy-start(s32[512]{0:T(512)} %param.12) | copy-start | bytes 6148
  19.2 11.8 %copy-start.4 = (s32[512,1]{0,1:T(1,128)S(1)}, s32[512,1]{0,1:T(1,128)}, u32[]{:S(2)}) copy-start(s32[512,1]{0,1:T(1,128)} %param.13) | copy-start | bytes 6148
  19.2 81.4 %all-to-all-start = ((bf16[128,176,128]{2,1,0:T(8,128)(2,1)}), bf16[128,176,128]{2,1,0:T(8,128)(2,1)}, u32[]{:S(2)}, u32[]{:S(2)}) async-start(bf16[128,176,128]{2,1,0:T(8,128)(2,1)} %fourier.1), calls=%async_computation | async-start | bytes 11534336 | tf_op jit(solution)/shard_map/all_to_all | solution.py:390
  108.2 29.2 %copy-start.1 = (bf16[1,366,548]{1,2,0:T(8,128)(2,1)S(1)}, bf16[1,366,548]{1,2,0:T(8,128)(2,1)}, u32[]{:S(2)}) copy-start(bf16[1,366,548]{1,2,0:T(8,128)(2,1)} %param.14) | copy-start | bytes 1203412
  108.2 29.2 %copy-start.2 = (f32[1,366]{1,0:T(1,128)S(1)}, f32[1,366]{1,0:T(1,128)}, u32[]{:S(2)}) copy-start(f32[1,366]{1,0:T(1,128)} %bias_ref.1) | copy-start | bytes 4396

commit v4 on v3

--- a/solution.py
+++ b/solution.py
@@ -313,51 +313,84 @@
     )(main_table, spot, row, coeff)
 
 
-def answer_kernel(state_ref, jac_ref, bias_ref, out_ref, jac_s):
+def jacobian_kernel(jac_ref, bias_ref, out_ref):
     channels = jac_ref.shape[1]
     levels = jac_ref.shape[0] // 4
-    rest = levels - LANES
-
-    @pl.when(pl.program_id(0) == 0)
-    def _():
-        jac = jac_ref[...].astype(F32)
-        jac_s[...] = jnp.zeros_like(jac_s)
-        for v in range(4):
-            at = v * levels
-            jac_s[v * LANES : (v + 1) * LANES, :] = jac[at : at + LANES].astype(BF16)
-            lo = 4 * LANES + (v % 2 * 2 + v // 2) * SLOT_LANES
-            piece = jnp.concatenate(
-                [jac[at + LANES : at + levels], jnp.zeros((16 - rest, channels), F32)], axis=0
-            )
-            jac_s[lo : lo + 16, :] = piece.astype(BF16)
-
-    depart = dot(state_ref[...], jac_s[...]) + bias_ref[...]
-    weighted = (depart / jnp.sqrt(1.0 + depart * depart * 0.25)).astype(BF16)
-    out_ref[:, :channels] = depart.astype(BF16)
-    out_ref[:, 3 * LANES : 3 * LANES + jac_ref.shape[0]] = lax.dot_general(
-        weighted, jac_ref[...], (((1,), (1,)), ((), ())), preferred_element_type=F32
-    ).astype(BF16)
-
-
-def answers(states, jac_t, bias):
-    total, lanes = states.shape
-    width, channels = jac_t.shape
-    out_lanes = -(-channels // LANES) * LANES + -(-width // LANES) * LANES
-    steps = 2
+    jac = jac_ref[...].astype(F32)
+    out_ref[...] = jnp.zeros_like(out_ref)
+    for v in range(4):
+        at = v * levels
+        out_ref[v * LANES : (v + 1) * LANES, :] = jac[at : at + LANES].astype(BF16)
+        lo = 4 * LANES + (v % 2 * 2 + v // 2) * SLOT_LANES
+        pad = jnp.zeros((16 - (levels - LANES), channels), F32)
+        piece = jnp.concatenate([jac[at + LANES : at + levels], pad], axis=0)
+        out_ref[lo : lo + 16, :] = piece.astype(BF16)
+    parts = []
+    left = bias_ref[...]
+    for _ in range(3):
+        parts.append(left.astype(BF16).astype(F32))
+        left = left - parts[-1]
+    parts.append(jnp.zeros((13, channels), F32))
+    out_ref[5 * LANES :, :] = jnp.concatenate(parts, axis=0).astype(BF16)
+
+
+def owner_table(jac_t, bias):
+    return pl.pallas_call(
+        jacobian_kernel,
+        out_shape=jax.ShapeDtypeStruct((5 * LANES + 16, jac_t.shape[1]), BF16),
+        compiler_params=pltpu.CompilerParams(vmem_limit_bytes=16 << 20),
+        name="jacobians",
+    )(jac_t, bias)
+
+
+def answer_kernel(place_ref, state_ref, own_ref, other_ref, out_ref):
+    width = 5 * LANES
+    sources = state_ref.shape[0]
+    channels = own_ref.shape[2]
+    rows = sources * 8
+    first = place_ref[1] == 0
+    states = state_ref[...].astype(F32)
+    low, high = states[:, :8].reshape(rows, width), states[:, 8:].reshape(rows, width)
+
+    def answer(state, jac_ref):
+        bias = jnp.sum(jac_ref[0, width:, :].astype(F32), axis=0, keepdims=True)
+        depart = dot(state.astype(BF16), jac_ref[0, :width, :]) + bias
+        weighted = (depart / jnp.sqrt(1.0 + depart * depart * 0.25)).astype(BF16)
+        grad = lax.dot_general(
+            weighted, jac_ref[0, :width, :], (((1,), (1,)), ((), ())), preferred_element_type=F32
+        )
+        return depart, grad
+
+    own = answer(jnp.where(first, low, high), own_ref)
+    other = answer(jnp.where(first, high, low), other_ref)
+    for part, at in ((0, 0), (1, 3 * LANES)):
+        size = own[part].shape[1]
+        low = jnp.where(first, own[part], other[part]).reshape(sources, 8, size)
+        high = jnp.where(first, other[part], own[part]).reshape(sources, 8, size)
+        both = jnp.concatenate([low, high], axis=1)
+        out_ref[:, :, at : at + size] = both.astype(BF16)
+
+
+def answers(states, place, own, other):
+    sources, rows, width = states.shape
+    chips, depth, channels = own.shape
+    pick = lambda g, place: ((place[0] - g + chips) % chips, 0, 0)
     return pl.pallas_call(
         answer_kernel,
-        out_shape=jax.ShapeDtypeStruct((total, out_lanes), BF16),
-        grid=(steps,),
-        in_specs=[
-            pl.BlockSpec((total // steps, lanes), lambda g: (g, 0)),
-            pl.BlockSpec((width, channels), lambda g: (0, 0)),
-            pl.BlockSpec((1, channels), lambda g: (0, 0)),
-        ],
-        out_specs=pl.BlockSpec((total // steps, out_lanes), lambda g: (g, 0)),
-        scratch_shapes=[pltpu.VMEM((lanes, channels), BF16)],
+        out_shape=jax.ShapeDtypeStruct((sources, rows, 8 * LANES), BF16),
+        grid_spec=pltpu.PrefetchScalarGridSpec(
+            num_scalar_prefetch=1,
+            grid=(chips,),
+            in_specs=[
+                pl.BlockSpec((sources, rows // chips, width), lambda g, place: (0, g, 0)),
+                pl.BlockSpec((1, depth, channels), pick),
+                pl.BlockSpec((1, depth, channels), pick),
+            ],
+            out_specs=pl.BlockSpec((sources, rows // chips, 8 * LANES), lambda g, place: (0, g, 0)),
+        ),
         compiler_params=pltpu.CompilerParams(vmem_limit_bytes=20 << 20),
         name="answers",
-    )(states, jac_t, bias)
+    )(place, states, own, other)
 
 
 def collect_kernel(spot_ref, back_ref, depart_ref, grad_ref):
@@ -370,7 +403,13 @@
     width = grad_ref.shape[0]
     both = jnp.transpose(dot(place, back_ref[...]))
     depart_ref[...] = both[:channels].astype(BF16)
-    grad_ref[...] = both[3 * LANES : 3 * LANES + width].astype(BF16)
+    levels = width // 4
+    parts = []
+    for v in range(4):
+        lo = 7 * LANES + (v % 2 * 2 + v // 2) * SLOT_LANES
+        parts.append(both[(3 + v) * LANES : (4 + v) * LANES])
+        parts.append(both[lo : lo + levels - LANES])
+    grad_ref[...] = jnp.concatenate(parts, axis=0).astype(BF16)
 
 
 def collect(spot, back, channels, width):
@@ -386,8 +425,15 @@
     )(spot, back)
 
 
-def exchange(x):
-    return lax.all_to_all(x, ("wave", "lat"), split_axis=0, concat_axis=0, tiled=True)
+def exchange(x, axes):
+    return lax.all_to_all(x, axes, split_axis=0, concat_axis=0, tiled=True)
+
+
+def chip_tables(table, lat_count):
+    ring = lambda step: [(i, (i + 2 * step) % lat_count) for i in range(lat_count)]
+    parts = [table] + [lax.ppermute(table, "lat", ring(step)) for step in range(1, lat_count // 2)]
+    own = pltpu.with_memory_space_constraint(jnp.stack(parts), pltpu.HBM)
+    return own, lax.ppermute(own, "lat", [(i, i ^ 1) for i in range(lat_count)])
 
 
 def local(control, spread, vertical, legendre, column_index, column_owner, jacobian, channel_bias):
@@ -403,13 +449,15 @@
     main_table, row, spot = tables(
         index, column_owner.reshape(1, cols), 4 * pairs * wave_count, slots
     )
-    coeff = exchange(blocks).reshape(wave_count, -1, LANES)
+    lat = lax.axis_index("lat").astype(jnp.int32)
+    jac_t = jnp.transpose(jacobian[0])
+    own, other = chip_tables(owner_table(jac_t, channel_bias), lax.axis_size("lat"))
+    coeff = exchange(blocks, ("wave", "lat")).reshape(wave_count, -1, LANES)
     outgoing = column_states(coeff, main_table, spot, row, slots)
     lanes = outgoing.shape[1]
-    states = exchange(outgoing.reshape(device_count, slots, lanes))
-    jac_t = jnp.transpose(jacobian[0])
-    reply = answers(states.reshape(device_count * slots, lanes), jac_t, channel_bias)
-    back = exchange(reply.reshape(device_count, slots, reply.shape[1]))
+    states = exchange(outgoing.reshape(wave_count, -1, lanes), "wave")
+    reply = answers(states, jnp.stack([lat // 2, lat % 2]), own, other)
+    back = exchange(reply, "wave")
     departures, increments = collect(
         spot, back.reshape(device_count * slots, -1), jac_t.shape[1], jac_t.shape[0]
     )

time: 178 us -> 201 us (1.13)
  waiting for transfers between devices: 66.9 us -> 104 us
  blocking collectives: 63.9 us -> 29.5 us
  starting transfers between devices: 11.8 us -> 23.7 us
  Pallas kernels: 29.8 us -> 34.5 us
    ppermute x0 -> x4, waiting for transfers between devices: none -> 84.5 us  [the longest x3 84.5 us: chip_tables(): lax.ppermute(table, 'lat', ring(step))]
    all_to_all x1 -> x2, waiting for transfers between devices: 66.9 us -> 19.9 us  [exchange(): return lax.all_to_all(x, axes, split_axis=0, concat_axis=0, tiled=True)]
    all_to_all x2 -> x1, blocking collectives: 63.9 us -> 29.5 us  [exchange(): return lax.all_to_all(x, axes, split_axis=0, concat_axis=0, tiled=True)]
    all_to_all x1 -> x2, starting transfers between devices: 11.8 us -> 18 us  [exchange(): return lax.all_to_all(x, axes, split_axis=0, concat_axis=0, tiled=True)]
    ppermute x0 -> x4, starting transfers between devices: none -> 5.79 us  [the longest x3 5.4 us: chip_tables(): lax.ppermute(table, 'lat', ring(step))]
    pallas_call x1 -> x2, Pallas kernels: 2.59 us -> 6.09 us  [the longest x1 5.95 us: answers(): pl.pallas_call(answer_kernel, out_shape=jax.ShapeDtypeStruct((sources, ro...]
  transfers between devices with their start and end apart: 1 -> 6, of which waited for: 1 -> 4; matrix products, arithmetic and copies ran while one was open for 0% -> 1% of each run, Pallas kernels for 2% -> 6%
where the time goes in v4:
time: 201 us; the launch traced here: 199 us
  waiting for transfers between devices  104 us (52%)
  Pallas kernels  34.5 us (17%)
  blocking collectives  29.5 us (15%)
  starting transfers between devices  23.7 us (12%)
  local copies, waits for them, and re-layouts  4.16 us (2%)
    ppermute x3, waiting for transfers between devices, chip_tables(): lax.ppermute(table, 'lat', ring(step))  84.5 us
    all_to_all x1, blocking collectives, exchange(): return lax.all_to_all(x, axes, split_axis=0, concat_axis=0, tiled=True)  29.5 us
    all_to_all x2, waiting for transfers between devices, exchange(): return lax.all_to_all(x, axes, split_axis=0, concat_axis=0, tiled=True)  19.9 us
    all_to_all x2, starting transfers between devices, exchange(): return lax.all_to_all(x, axes, split_axis=0, concat_axis=0, tiled=True)  18 us
    pallas_call x1, Pallas kernels, fourier_blocks(): pl.pallas_call(fourier_kernel, out_shape=jax.ShapeDtypeStruct((dests, 32...  14.3 us
    pallas_call x1, Pallas kernels, column_states(): pl.pallas_call(state_kernel, out_shape=jax.ShapeDtypeStruct((total, 5 * L...  8.73 us
    pallas_call x1, Pallas kernels, answers(): pl.pallas_call(answer_kernel, out_shape=jax.ShapeDtypeStruct((sources, ro...  5.95 us
    ppermute x3, starting transfers between devices, chip_tables(): lax.ppermute(table, 'lat', ring(step))  5.4 us
  transfers between devices with their start and end apart: 6, of which 4 were waited for; matrix products, arithmetic and copies ran while one was open for 1% of the time, Pallas kernels for 6%

profile of v4, /device:TPU:1, one launch (start us, length us, event | category | flops | bytes accessed | tf_op | source)
XLA Modules:
  0.0 198.9 jit_solution(4235912263095195179)
XLA Ops:
  0.6 0.0 copy-start
  0.7 1.3 copy-done
  2.0 0.3 constant_dynamic-slice_fusion.1
  2.3 0.8 copy.16
  3.1 1.1 constant_dynamic-slice_fusion
  4.2 0.6 copy.17
  4.8 14.3 %fourier.1 = bf16[128,176,128]{2,1,0:T(8,128)(2,1)} custom-call(s32[1]{0:T(128)} %bitcast.4.base_ref, bf16[20,1,137,641]{3,2,1,0:T(8,128)(2,1)} %bitcast.31, f32[137,640]{1,0:T(8,128)} %bitcast.32, bf16[137,137]{1,0:T(8,128)(2,1)} %bitcast.36, bf16[20,641,512]{2,1,0:T(8,128)(2,1)} %leg_ref.1), custom_call_target="tpu_custom_call" | custom-call | tf_op jit(solution)/shard_map/fourier/pallas_call | solution.py:151
  19.1 0.0 copy-start.1
  19.1 0.0 copy-start.2
  19.1 11.8 %all-to-all-start = ((bf16[128,176,128]{2,1,0:T(8,128)(2,1)}), bf16[128,176,128]{2,1,0:T(8,128)(2,1)}, u32[]{:S(2)}, u32[]{:S(2)}) async-start(bf16[128,176,128]{2,1,0:T(8,128)(2,1)} %fourier.1), calls=%async_computation | async-start | bytes 11534336 | tf_op jit(solution)/shard_map/all_to_all | solution.py:429
  30.9 0.0 copy-done.1
  30.9 0.0 copy-done.2
  30.9 0.1 jacobians.1
  31.1 1.5 collective-permute-start
  32.6 2.9 %collective-permute-start.1 = (bf16[656,366]{1,0:T(8,128)(2,1)S(1)}, bf16[656,366]{1,0:T(8,128)(2,1)S(1)}, u32[]{:S(2)}, u32[]{:S(2)}) collective-permute-start(bf16[656,366]{1,0:T(8,128)(2,1)S(1)} %jacobians.1), channel_id=1, source_target_pairs={{0,4},{1,5},{2,6},{3,7},{4,0},{5,1},{6,2},{7,3},{8,12},{9,13},{10,... | collective-permute-start | bytes 1440584 | tf_op jit(solution)/shard_map/ppermute | solution.py:434
  35.6 0.9 collective-permute-start.2
  36.5 70.2 %collective-permute-done = bf16[656,366]{1,0:T(8,128)(2,1)S(1)} collective-permute-done((bf16[656,366]{1,0:T(8,128)(2,1)S(1)}, bf16[656,366]{1,0:T(8,128)(2,1)S(1)}, u32[]{:S(2)}, u32[]{:S(2)}) %collective-permute-start) | collective-permute-done | bytes 480224 | tf_op jit(solution)/shard_map/ppermute | solution.py:434
  106.7 11.8 %collective-permute-done.1 = bf16[656,366]{1,0:T(8,128)(2,1)S(1)} collective-permute-done((bf16[656,366]{1,0:T(8,128)(2,1)S(1)}, bf16[656,366]{1,0:T(8,128)(2,1)S(1)}, u32[]{:S(2)}, u32[]{:S(2)}) %collective-permute-start.1) | collective-permute-done | bytes 480224 | tf_op jit(solution)/shard_map/ppermute | solution.py:434
  118.5 2.4 %collective-permute-done.2 = bf16[656,366]{1,0:T(8,128)(2,1)S(1)} collective-permute-done((bf16[656,366]{1,0:T(8,128)(2,1)S(1)}, bf16[656,366]{1,0:T(8,128)(2,1)S(1)}, u32[]{:S(2)}, u32[]{:S(2)}) %collective-permute-start.2) | collective-permute-done | bytes 480224 | tf_op jit(solution)/shard_map/ppermute | solution.py:434
  120.9 0.0 copy-start.3
  120.9 0.0 copy-start.4
  120.9 1.9 pad_maximum_fusion.own_ref
  122.8 0.4 collective-permute-start.3
  123.2 0.0 copy-done.3
  123.2 0.0 copy-done.4
  123.2 2.7 %tables.1 = (bf16[512,1280]{1,0:T(8,128)(2,1)S(1)}, f32[512,128]{1,0:T(8,128)S(1)}, s32[1,512]{1,0:T(1,128)S(1)}) custom-call(s32[1,512]{1,0:T(1,128)S(1)} %bitcast.29, s32[1,512]{1,0:T(1,128)S(1)} %bitcast.30), custom_call_target="tpu_custom_call" | custom-call | flops 39321600 | bytes 4194304 | tf_op jit(solution)/shard_map/tables/pallas_call | solution.py:227
  125.9 0.0 all-to-all-done
  125.9 8.7 %states.1 = bf16[1024,640]{1,0:T(8,128)(2,1)} custom-call(bf16[512,1280]{1,0:T(8,128)(2,1)S(1)} %get-tuple-element.8.main_ref, s32[1,512]{1,0:T(1,128)S(1)} %get-tuple-element.7.spot_ref, f32[512,128]{1,0:T(8,128)S(1)} %get-tuple-element.9.row_ref, bf16[16,1408,128]{2,1,0:T(8,128)(2,1)} %bitcast.9.coeff_ref), custom_call_target="tpu_custom_call" | custom-call | tf_op jit(solution)/shard_map/states/pallas_call | solution.py:294
  134.7 6.2 %all-to-all-start.1 = ((bf16[16,64,640]{2,1,0:T(8,128)(2,1)}), bf16[16,64,640]{2,1,0:T(8,128)(2,1)S(1)}, u32[]{:S(2)}, u32[]{:S(2)}) async-start(bf16[16,64,640]{2,1,0:T(8,128)(2,1)} %bitcast.10), calls=%async_computation.1 | async-start | bytes 2621440 | tf_op jit(solution)/shard_map/all_to_all | solution.py:429
  140.8 0.1 pad_add_fusion.place_ref
  140.9 0.0 collective-permute-done.3.other_ref
  140.9 19.9 %all-to-all-done.1.state_ref = bf16[16,64,640]{2,1,0:T(8,128)(2,1)S(1)} async-done(((bf16[16,64,640]{2,1,0:T(8,128)(2,1)}), bf16[16,64,640]{2,1,0:T(8,128)(2,1)S(1)}, u32[]{:S(2)}, u32[]{:S(2)}) %all-to-all-start.1) | async-done | bytes 1310752 | tf_op jit(solution)/shard_map/all_to_all | solution.py:429
  160.8 5.9 %answers.1 = bf16[16,64,1024]{2,1,0:T(8,128)(2,1)S(1)} custom-call(s32[2]{0:T(128)S(1)} %pad_add_fusion.place_ref, bf16[16,64,640]{2,1,0:T(8,128)(2,1)S(1)} %all-to-all-done.1.state_ref, bf16[4,656,366]{2,1,0:T(8,128)(2,1)} %pad_maximum_fusion.own_ref, bf16[4,656,366]{2,1,0:T(8,128)(2,1)} %collective-permute-done.3.other_ref), custom_call_target="tpu_custom_call" | custom-call | tf_op jit(solution)/shard_map/answers/pallas_call | solution.py:378
  166.7 29.5 %all_to_all.15 = bf16[16,64,1024]{2,1,0:T(8,128)(2,1)S(1)} all-to-all(bf16[16,64,1024]{2,1,0:T(8,128)(2,1)S(1)} %answers.1), channel_id=1, replica_groups=mesh['wave'=16,'lat'=8] {'wave'}, dimensions={0} | all-to-all | bytes 4194304 | tf_op jit(solution)/shard_map/all_to_all | solution.py:429
  196.3 2.7 %collect.1 = (bf16[366,512]{1,0:T(8,128)(2,1)}, bf16[548,512]{1,0:T(8,128)(2,1)}) custom-call(s32[1,512]{1,0:T(1,128)S(1)} %get-tuple-element.7.spot_ref, bf16[1024,1024]{1,0:T(8,128)(2,1)S(1)} %bitcast.26), custom_call_target="tpu_custom_call" | custom-call | tf_op jit(solution)/shard_map/collect/pallas_call | solution.py:417
Async XLA Ops:
  0.6 1.4 copy-start
  19.1 11.8 %copy-start.1 = (bf16[1,366,548]{1,2,0:T(8,128)(2,1)S(1)}, bf16[1,366,548]{1,2,0:T(8,128)(2,1)}, u32[]{:S(2)}) copy-start(bf16[1,366,548]{1,2,0:T(8,128)(2,1)} %param.14) | copy-start | bytes 1203412
  19.1 11.8 %copy-start.2 = (f32[1,366]{1,0:T(1,128)S(1)}, f32[1,366]{1,0:T(1,128)}, u32[]{:S(2)}) copy-start(f32[1,366]{1,0:T(1,128)} %bias_ref.1) | copy-start | bytes 4396
  19.1 106.8 %all-to-all-start = ((bf16[128,176,128]{2,1,0:T(8,128)(2,1)}), bf16[128,176,128]{2,1,0:T(8,128)(2,1)}, u32[]{:S(2)}, u32[]{:S(2)}) async-start(bf16[128,176,128]{2,1,0:T(8,128)(2,1)} %fourier.1), calls=%async_computation | async-start | bytes 11534336 | tf_op jit(solution)/shard_map/all_to_all | solution.py:429
  31.1 75.6 %collective-permute-start = (bf16[656,366]{1,0:T(8,128)(2,1)S(1)}, bf16[656,366]{1,0:T(8,128)(2,1)S(1)}, u32[]{:S(2)}, u32[]{:S(2)}) collective-permute-start(bf16[656,366]{1,0:T(8,128)(2,1)S(1)} %jacobians.1), channel_id=1, source_target_pairs={{0,2},{1,3},{2,4},{3,5},{4,6},{5,7},{6,0},{7,1},{8,10},{9,11},{10,... | collective-permute-start | bytes 1440584 | tf_op jit(solution)/shard_map/ppermute | solution.py:434
  32.6 85.9 %collective-permute-start.1 = (bf16[656,366]{1,0:T(8,128)(2,1)S(1)}, bf16[656,366]{1,0:T(8,128)(2,1)S(1)}, u32[]{:S(2)}, u32[]{:S(2)}) collective-permute-start(bf16[656,366]{1,0:T(8,128)(2,1)S(1)} %jacobians.1), channel_id=1, source_target_pairs={{0,4},{1,5},{2,6},{3,7},{4,0},{5,1},{6,2},{7,3},{8,12},{9,13},{10,... | collective-permute-start | bytes 1440584 | tf_op jit(solution)/shard_map/ppermute | solution.py:434
  35.6 85.4 %collective-permute-start.2 = (bf16[656,366]{1,0:T(8,128)(2,1)S(1)}, bf16[656,366]{1,0:T(8,128)(2,1)S(1)}, u32[]{:S(2)}, u32[]{:S(2)}) collective-permute-start(bf16[656,366]{1,0:T(8,128)(2,1)S(1)} %jacobians.1), channel_id=1, source_target_pairs={{0,6},{1,7},{2,0},{3,1},{4,2},{5,3},{6,4},{7,5},{8,14},{9,15},{10,... | collective-permute-start | bytes 1440584 | tf_op jit(solution)/shard_map/ppermute | solution.py:434
  120.9 2.3 %copy-start.3 = (s32[512]{0:T(512)S(1)}, s32[512]{0:T(512)}, u32[]{:S(2)}) copy-start(s32[512]{0:T(512)} %param.12) | copy-start | bytes 6148
  120.9 2.3 %copy-start.4 = (s32[512,1]{0,1:T(1,128)S(1)}, s32[512,1]{0,1:T(1,128)}, u32[]{:S(2)}) copy-start(s32[512,1]{0,1:T(1,128)} %param.13) | copy-start | bytes 6148
  122.8 18.1 %collective-permute-start.3 = (bf16[4,656,366]{2,1,0:T(8,128)(2,1)}, bf16[4,656,366]{2,1,0:T(8,128)(2,1)}, u32[]{:S(2)}, u32[]{:S(2)}) collective-permute-start(bf16[4,656,366]{2,1,0:T(8,128)(2,1)} %pad_maximum_fusion.own_ref), channel_id=1, source_target_pairs={{0,1},{1,0},{2,3},{3,2},{4,5},{5,4},{6,7},{7,6},{8,9},{9,8},{10,11... | collective-permute-start | bytes 5762312 | tf_op jit(solution)/shard_map/ppermute | solution.py:436
  134.7 26.1 %all-to-all-start.1 = ((bf16[16,64,640]{2,1,0:T(8,128)(2,1)}), bf16[16,64,640]{2,1,0:T(8,128)(2,1)S(1)}, u32[]{:S(2)}, u32[]{:S(2)}) async-start(bf16[16,64,640]{2,1,0:T(8,128)(2,1)} %bitcast.10), calls=%async_computation.1 | async-start | bytes 2621440 | tf_op jit(solution)/shard_map/all_to_all | solution.py:429

commit v5 on v4

--- a/solution.py
+++ b/solution.py
@@ -6,7 +6,7 @@
 from jax import lax
 from jax.experimental import pallas as pl
 from jax.experimental.pallas import tpu as pltpu
-from jax.sharding import PartitionSpec as P
+from jax.sharding import Mesh, PartitionSpec as P
 
 NLON = 2560
 LANES = 128
@@ -343,21 +343,20 @@
     )(jac_t, bias)
 
 
-def answer_kernel(place_ref, state_ref, own_ref, other_ref, out_ref):
+def answer_kernel(core_ref, state_ref, own_ref, other_ref, out_ref):
     width = 5 * LANES
     sources = state_ref.shape[0]
-    channels = own_ref.shape[2]
     rows = sources * 8
-    first = place_ref[1] == 0
+    first = core_ref[0] == 0
     states = state_ref[...].astype(F32)
     low, high = states[:, :8].reshape(rows, width), states[:, 8:].reshape(rows, width)
 
     def answer(state, jac_ref):
-        bias = jnp.sum(jac_ref[0, width:, :].astype(F32), axis=0, keepdims=True)
-        depart = dot(state.astype(BF16), jac_ref[0, :width, :]) + bias
+        bias = jnp.sum(jac_ref[width:, :].astype(F32), axis=0, keepdims=True)
+        depart = dot(state.astype(BF16), jac_ref[:width, :]) + bias
         weighted = (depart / jnp.sqrt(1.0 + depart * depart * 0.25)).astype(BF16)
         grad = lax.dot_general(
-            weighted, jac_ref[0, :width, :], (((1,), (1,)), ((), ())), preferred_element_type=F32
+            weighted, jac_ref[:width, :], (((1,), (1,)), ((), ())), preferred_element_type=F32
         )
         return depart, grad
 
@@ -371,26 +370,23 @@
         out_ref[:, :, at : at + size] = both.astype(BF16)
 
 
-def answers(states, place, own, other):
+def answers(states, core, own, other):
     sources, rows, width = states.shape
-    chips, depth, channels = own.shape
-    pick = lambda g, place: ((place[0] - g + chips) % chips, 0, 0)
+    steps = 2
     return pl.pallas_call(
         answer_kernel,
         out_shape=jax.ShapeDtypeStruct((sources, rows, 8 * LANES), BF16),
-        grid_spec=pltpu.PrefetchScalarGridSpec(
-            num_scalar_prefetch=1,
-            grid=(chips,),
-            in_specs=[
-                pl.BlockSpec((sources, rows // chips, width), lambda g, place: (0, g, 0)),
-                pl.BlockSpec((1, depth, channels), pick),
-                pl.BlockSpec((1, depth, channels), pick),
-            ],
-            out_specs=pl.BlockSpec((sources, rows // chips, 8 * LANES), lambda g, place: (0, g, 0)),
-        ),
+        grid=(steps,),
+        in_specs=[
+            pl.BlockSpec(memory_space=pltpu.SMEM),
+            pl.BlockSpec((sources // steps, rows, width), lambda g: (g, 0, 0)),
+            pl.BlockSpec(own.shape, lambda g: (0, 0)),
+            pl.BlockSpec(own.shape, lambda g: (0, 0)),
+        ],
+        out_specs=pl.BlockSpec((sources // steps, rows, 8 * LANES), lambda g: (g, 0, 0)),
         compiler_params=pltpu.CompilerParams(vmem_limit_bytes=20 << 20),
         name="answers",
-    )(place, states, own, other)
+    )(core, states, own, other)
 
 
 def collect_kernel(spot_ref, back_ref, depart_ref, grad_ref):
@@ -429,35 +425,28 @@
     return lax.all_to_all(x, axes, split_axis=0, concat_axis=0, tiled=True)
 
 
-def chip_tables(table, lat_count):
-    ring = lambda step: [(i, (i + 2 * step) % lat_count) for i in range(lat_count)]
-    parts = [table] + [lax.ppermute(table, "lat", ring(step)) for step in range(1, lat_count // 2)]
-    own = pltpu.with_memory_space_constraint(jnp.stack(parts), pltpu.HBM)
-    return own, lax.ppermute(own, "lat", [(i, i ^ 1) for i in range(lat_count)])
-
-
 def local(control, spread, vertical, legendre, column_index, column_owner, jacobian, channel_bias):
     pairs = control.shape[0]
     wave_count = lax.axis_size("wave")
-    device_count = wave_count * lax.axis_size("lat")
+    device_count = wave_count * lax.axis_size("z") * lax.axis_size("core")
     cols = column_index.shape[0]
     slots = max(2, 2 * cols // device_count)
-    var = lax.axis_index("lat") // 2
+    var = lax.axis_index("z")
     pair_base = (lax.axis_index("wave") * pairs).astype(jnp.int32).reshape(1)
     blocks = fourier_blocks(control, spread[var], vertical[var], legendre, pair_base, device_count)
     index = column_index.reshape(1, cols)
     main_table, row, spot = tables(
         index, column_owner.reshape(1, cols), 4 * pairs * wave_count, slots
     )
-    lat = lax.axis_index("lat").astype(jnp.int32)
     jac_t = jnp.transpose(jacobian[0])
-    own, other = chip_tables(owner_table(jac_t, channel_bias), lax.axis_size("lat"))
-    coeff = exchange(blocks, ("wave", "lat")).reshape(wave_count, -1, LANES)
+    own = owner_table(jac_t, channel_bias)
+    other = lax.ppermute(own, "core", [(0, 1), (1, 0)])
+    coeff = exchange(blocks, ("wave", "z", "core")).reshape(wave_count, -1, LANES)
     outgoing = column_states(coeff, main_table, spot, row, slots)
-    lanes = outgoing.shape[1]
-    states = exchange(outgoing.reshape(wave_count, -1, lanes), "wave")
-    reply = answers(states, jnp.stack([lat // 2, lat % 2]), own, other)
-    back = exchange(reply, "wave")
+    chips = device_count // 2
+    states = exchange(outgoing.reshape(chips, 2 * slots, outgoing.shape[1]), ("wave", "z"))
+    core = lax.axis_index("core").astype(jnp.int32).reshape(1)
+    back = exchange(answers(states, core, own, other), ("wave", "z"))
     departures, increments = collect(
         spot, back.reshape(device_count * slots, -1), jac_t.shape[1], jac_t.shape[0]
     )
@@ -465,19 +454,23 @@
 
 
 def solution(mesh):
+    waves, lats = mesh.devices.shape
+    split = Mesh(mesh.devices.reshape(waves, lats // 2, 2), ("wave", "z", "core"))
+    lat = ("z", "core")
+    everyone = ("wave", "z", "core")
     return jax.shard_map(
         local,
-        mesh=mesh,
+        mesh=split,
         in_specs=(
-            P("wave", None, "lat", None),
+            P("wave", None, lat, None),
             P(),
             P(),
             P("wave", None, None),
-            P(("wave", "lat")),
-            P(("wave", "lat"), None),
-            P(("wave", "lat"), None, None),
-            P(("wave", "lat"), None),
+            P(everyone),
+            P(everyone, None),
+            P(everyone, None, None),
+            P(everyone, None),
         ),
-        out_specs=(P(("wave", "lat"), None), P(("wave", "lat"), None)),
+        out_specs=(P(everyone, None), P(everyone, None)),
         check_vma=False,
     )

time: 201 us -> 179 us (0.89)
  waiting for transfers between devices: 104 us -> 84.7 us
  blocking collectives: 29.5 us -> 32.5 us
  starting transfers between devices: 23.7 us -> 21 us
  Pallas kernels: 34.5 us -> 32.3 us
    ppermute x4 -> x1, waiting for transfers between devices: 84.5 us -> 1.64 us  [local(): other = lax.ppermute(own, 'core', [(0, 1), (1, 0)])]
    all_to_all x2, waiting for transfers between devices: 19.9 us -> 83.1 us  [exchange(): return lax.all_to_all(x, axes, split_axis=0, concat_axis=0, tiled=True)]
    ppermute x4 -> x1, starting transfers between devices: 5.79 us -> 0.73 us  [local(): other = lax.ppermute(own, 'core', [(0, 1), (1, 0)])]
    all_to_all x1, blocking collectives: 29.5 us -> 32.5 us  [exchange(): return lax.all_to_all(x, axes, split_axis=0, concat_axis=0, tiled=True)]
    all_to_all x2, starting transfers between devices: 18 us -> 20.2 us  [exchange(): return lax.all_to_all(x, axes, split_axis=0, concat_axis=0, tiled=True)]
    pallas_call x1, Pallas kernels: 5.95 us -> 3.76 us  [answers(): pl.pallas_call(answer_kernel, out_shape=jax.ShapeDtypeStruct((sources, ro...]
  transfers between devices with their start and end apart: 6 -> 3, of which waited for: 4 -> 3; matrix products, arithmetic and copies ran while one was open for 1% -> 0% of each run, Pallas kernels for 6% -> 2%
where the time goes in v5:
time: 179 us; the launch traced here: 176 us
  waiting for transfers between devices  84.7 us (47%)
  blocking collectives  32.5 us (18%)
  Pallas kernels  32.3 us (18%)
  starting transfers between devices  21 us (12%)
  local copies, waits for them, and re-layouts  5.17 us (3%)
    all_to_all x2, waiting for transfers between devices, exchange(): return lax.all_to_all(x, axes, split_axis=0, concat_axis=0, tiled=True)  83.1 us
    all_to_all x1, blocking collectives, exchange(): return lax.all_to_all(x, axes, split_axis=0, concat_axis=0, tiled=True)  32.5 us
    all_to_all x2, starting transfers between devices, exchange(): return lax.all_to_all(x, axes, split_axis=0, concat_axis=0, tiled=True)  20.2 us
    pallas_call x1, Pallas kernels, fourier_blocks(): pl.pallas_call(fourier_kernel, out_shape=jax.ShapeDtypeStruct((dests, 32...  14.3 us
    pallas_call x1, Pallas kernels, column_states(): pl.pallas_call(state_kernel, out_shape=jax.ShapeDtypeStruct((total, 5 * L...  8.71 us
    pallas_call x1, Pallas kernels, answers(): pl.pallas_call(answer_kernel, out_shape=jax.ShapeDtypeStruct((sources, ro...  3.76 us
    unnamed x12, local copies, waits for them, and re-layouts  3.76 us
  transfers between devices with their start and end apart: 3, of which 3 were waited for; matrix products, arithmetic and copies ran while one was open for 0% of the time, Pallas kernels for 2%

profile of v5, /device:TPU:1, one launch (start us, length us, event | category | flops | bytes accessed | tf_op | source)
XLA Modules:
  0.0 176.3 jit_solution(6446960490145634777)
XLA Ops:
  0.6 0.0 copy-start
  0.7 1.3 copy-done
  2.0 0.3 constant_dynamic-slice_fusion.1
  2.3 0.8 copy.16
  3.1 1.1 constant_dynamic-slice_fusion
  4.2 0.6 copy.17
  4.8 14.3 %fourier.1 = bf16[128,176,128]{2,1,0:T(8,128)(2,1)} custom-call(s32[1]{0:T(128)} %bitcast.3.base_ref, bf16[20,1,137,641]{3,2,1,0:T(8,128)(2,1)} %bitcast.25, f32[137,640]{1,0:T(8,128)} %bitcast.26, bf16[137,137]{1,0:T(8,128)(2,1)} %bitcast.27, bf16[20,641,512]{2,1,0:T(8,128)(2,1)} %leg_ref.1), custom_call_target="tpu_custom_call" | custom-call | tf_op jit(solution)/shard_map/fourier/pallas_call | solution.py:151
  19.1 0.0 copy-start.3
  19.1 0.0 copy-start.4
  19.1 11.8 %all-to-all-start = ((bf16[128,176,128]{2,1,0:T(8,128)(2,1)}), bf16[128,176,128]{2,1,0:T(8,128)(2,1)}, u32[]{:S(2)}, u32[]{:S(2)}) async-start(bf16[128,176,128]{2,1,0:T(8,128)(2,1)} %fourier.1), calls=%async_computation | async-start | bytes 11534336 | tf_op jit(solution)/shard_map/all_to_all | solution.py:425
  30.9 0.0 copy-done.3
  30.9 0.0 copy-done.4
  30.9 2.7 %tables.1 = (bf16[512,1280]{1,0:T(8,128)(2,1)S(1)}, f32[512,128]{1,0:T(8,128)S(1)}, s32[1,512]{1,0:T(1,128)S(1)}) custom-call(s32[1,512]{1,0:T(1,128)S(1)} %bitcast.23, s32[1,512]{1,0:T(1,128)S(1)} %bitcast.24), custom_call_target="tpu_custom_call" | custom-call | flops 39321600 | bytes 4194304 | tf_op jit(solution)/shard_map/tables/pallas_call | solution.py:227
  33.6 66.9 %all-to-all-done = bf16[128,176,128]{2,1,0:T(8,128)(2,1)} async-done(((bf16[128,176,128]{2,1,0:T(8,128)(2,1)}), bf16[128,176,128]{2,1,0:T(8,128)(2,1)}, u32[]{:S(2)}, u32[]{:S(2)}) %all-to-all-start) | async-done | bytes 5767200 | tf_op jit(solution)/shard_map/all_to_all | solution.py:425
  100.5 8.7 %states.1 = bf16[1024,640]{1,0:T(8,128)(2,1)} custom-call(bf16[512,1280]{1,0:T(8,128)(2,1)S(1)} %get-tuple-element.8.main_ref, s32[1,512]{1,0:T(1,128)S(1)} %get-tuple-element.7.spot_ref, f32[512,128]{1,0:T(8,128)S(1)} %get-tuple-element.9.row_ref, bf16[16,1408,128]{2,1,0:T(8,128)(2,1)} %bitcast.8.coeff_ref), custom_call_target="tpu_custom_call" | custom-call | tf_op jit(solution)/shard_map/states/pallas_call | solution.py:294
  109.2 0.0 copy-start.2
  109.2 8.4 %all-to-all-start.1 = ((bf16[64,16,640]{2,1,0:T(8,128)(2,1)}), bf16[64,16,640]{2,1,0:T(8,128)(2,1)S(1)}, u32[]{:S(2)}, u32[]{:S(2)}) async-start(bf16[64,16,640]{2,1,0:T(8,128)(2,1)} %bitcast.9), calls=%async_computation.1 | async-start | bytes 2621440 | tf_op jit(solution)/shard_map/all_to_all | solution.py:425
  117.6 0.0 copy-done.2
  117.7 0.0 copy-start.1
  117.7 1.0 copy-done.1
  118.7 0.1 jacobians.1.own_ref
  118.8 0.7 collective-permute-start
  119.5 1.6 collective-permute-done.other_ref
  121.2 16.2 %all-to-all-done.1.state_ref = bf16[64,16,640]{2,1,0:T(8,128)(2,1)S(1)} async-done(((bf16[64,16,640]{2,1,0:T(8,128)(2,1)}), bf16[64,16,640]{2,1,0:T(8,128)(2,1)S(1)}, u32[]{:S(2)}, u32[]{:S(2)}) %all-to-all-start.1) | async-done | bytes 1310752 | tf_op jit(solution)/shard_map/all_to_all | solution.py:425
  137.4 3.8 %answers.1 = bf16[64,16,1024]{2,1,0:T(8,128)(2,1)S(1)} custom-call(s32[1]{0:T(128)} %bitcast.2.core_ref, bf16[64,16,640]{2,1,0:T(8,128)(2,1)S(1)} %all-to-all-done.1.state_ref, bf16[656,366]{1,0:T(8,128)(2,1)S(1)} %jacobians.1.own_ref, bf16[656,366]{1,0:T(8,128)(2,1)} %collective-permute-done.other_ref), custom_call_target="tpu_custom_call" | custom-call | tf_op jit(solution)/shard_map/answers/pallas_call | solution.py:376
  141.2 32.5 %all_to_all.15 = bf16[64,16,1024]{2,1,0:T(8,128)(2,1)S(1)} all-to-all(bf16[64,16,1024]{2,1,0:T(8,128)(2,1)S(1)} %answers.1), channel_id=1, replica_groups=mesh['wave'=16,'z'=4,'core'=2] {'wave','z'}, dimensions={0} | all-to-all | bytes 4194304 | tf_op jit(solution)/shard_map/all_to_all | solution.py:425
  173.7 2.7 %collect.1 = (bf16[366,512]{1,0:T(8,128)(2,1)}, bf16[548,512]{1,0:T(8,128)(2,1)}) custom-call(s32[1,512]{1,0:T(1,128)S(1)} %get-tuple-element.7.spot_ref, bf16[1024,1024]{1,0:T(8,128)(2,1)S(1)} %bitcast.21), custom_call_target="tpu_custom_call" | custom-call | tf_op jit(solution)/shard_map/collect/pallas_call | solution.py:413
Async XLA Ops:
  0.6 1.4 copy-start
  19.1 11.8 %copy-start.3 = (s32[512]{0:T(512)S(1)}, s32[512]{0:T(512)}, u32[]{:S(2)}) copy-start(s32[512]{0:T(512)} %param.12) | copy-start | bytes 6148
  19.1 11.8 %copy-start.4 = (s32[512,1]{0,1:T(1,128)S(1)}, s32[512,1]{0,1:T(1,128)}, u32[]{:S(2)}) copy-start(s32[512,1]{0,1:T(1,128)} %param.13) | copy-start | bytes 6148
  19.1 81.4 %all-to-all-start = ((bf16[128,176,128]{2,1,0:T(8,128)(2,1)}), bf16[128,176,128]{2,1,0:T(8,128)(2,1)}, u32[]{:S(2)}, u32[]{:S(2)}) async-start(bf16[128,176,128]{2,1,0:T(8,128)(2,1)} %fourier.1), calls=%async_computation | async-start | bytes 11534336 | tf_op jit(solution)/shard_map/all_to_all | solution.py:425
  109.2 8.5 %copy-start.2 = (f32[1,366]{1,0:T(1,128)S(1)}, f32[1,366]{1,0:T(1,128)}, u32[]{:S(2)}) copy-start(f32[1,366]{1,0:T(1,128)} %bias_ref.1) | copy-start | bytes 4396
  109.2 28.2 %all-to-all-start.1 = ((bf16[64,16,640]{2,1,0:T(8,128)(2,1)}), bf16[64,16,640]{2,1,0:T(8,128)(2,1)S(1)}, u32[]{:S(2)}, u32[]{:S(2)}) async-start(bf16[64,16,640]{2,1,0:T(8,128)(2,1)} %bitcast.9), calls=%async_computation.1 | async-start | bytes 2621440 | tf_op jit(solution)/shard_map/all_to_all | solution.py:425
  117.7 1.0 copy-start.1
  118.8 2.4 %collective-permute-start = (bf16[656,366]{1,0:T(8,128)(2,1)S(1)}, bf16[656,366]{1,0:T(8,128)(2,1)}, u32[]{:S(2)}, u32[]{:S(2)}) collective-permute-start(bf16[656,366]{1,0:T(8,128)(2,1)S(1)} %jacobians.1.own_ref), channel_id=1, source_target_pairs={{0,1},{1,0},{2,3},{3,2},{4,5},{5,4},{6,7},{7,6},{8,9},{9,8},{10,11... | collective-permute-start | bytes 1440584 | tf_op jit(solution)/shard_map/ppermute | solution.py:443

commit v6 on v3

--- a/solution.py
+++ b/solution.py
@@ -31,6 +31,8 @@
     main_s,
     rest_s,
     rem_s,
+    leg_s,
+    leg_sem,
     spread_s,
     second_s,
     first_s,
@@ -44,9 +46,16 @@
     rows = leg_ref.shape[2]
     dests = out_ref.shape[0]
     steps = pl.num_programs(0) - 3
+    depth = leg_s.shape[0]
     t = pl.program_id(0)
     lane = lax.broadcasted_iota(jnp.int32, (1, LANES), 1)
     slot = lax.broadcasted_iota(jnp.int32, (1, slots), 1)
+
+    def fetch(step):
+        at = step % depth
+        return pltpu.make_async_copy(
+            leg_ref.at[pl.ds(4 * step, 4)], leg_s.at[at], leg_sem.at[at]
+        )
 
     def align(step):
         pair = base_ref[0] + step * 4
@@ -90,12 +99,12 @@
         both = jnp.concatenate(
             [jnp.where(keep, mixed, zero), jnp.where(keep, zero, mixed)], axis=0
         )
-        both = dot(both, leg_ref[i, lo:hi, :])
+        both = dot(both, leg_s[(t - 1) % depth, i, lo:hi, :])
         half_rows = spec.shape[0]
-        first = both[:half_rows] + dot(spec[:, :lo], leg_ref[i, :lo, :])
+        first = both[:half_rows] + dot(spec[:, :lo], leg_s[(t - 1) % depth, i, :lo, :])
         second = both[half_rows:]
         if not early:
-            second = second + dot(spec[:, hi:], leg_ref[i, hi:, :])
+            second = second + dot(spec[:, hi:], leg_s[(t - 1) % depth, i, hi:, :])
         parts = (first, second)
         for h in range(2):
             j = 2 * i + h
@@ -107,16 +116,29 @@
 
     @pl.when(t == 0)
     def _():
+        for step in range(depth):
+            fetch(step).start()
+        mine = lax.broadcasted_iota(jnp.int32, (1, 4, 1), 1) == base_ref[1]
+        spread = jnp.sum(jnp.where(mine, spread_ref[...], 0.0), axis=1)
         spread_s[:, waves:] = jnp.zeros((modes, spread_s.shape[1] - waves), F32)
-        spread_s[:, :waves] = spread_ref[...]
-        second_s[:, :waves] = pltpu.roll(spread_ref[...], 1, 1)
-        second_s[:, waves : waves + 1] = spread_ref[:, waves - 1 :]
+        spread_s[:, :waves] = spread
+        second_s[:, :waves] = pltpu.roll(spread, 1, 1)
+        second_s[:, waves : waves + 1] = spread[:, waves - 1 :]
+        vert = jnp.sum(jnp.where(mine, vert_ref[...].astype(F32), 0.0), axis=1)
         vert_s[...] = jnp.zeros_like(vert_s)
-        vert_s[:modes, :] = vert_ref[...]
+        vert_s[:modes, :] = vert.astype(BF16)
         rem_s[...] = jnp.zeros_like(rem_s)
         align(0)
         for i in range(4):
             scale(0, i)
+
+    @pl.when((t > 0) & (t <= steps))
+    def _():
+        fetch(t - 1).wait()
+
+    @pl.when((t > 1) & (t - 2 + depth < steps))
+    def _():
+        fetch(t - 2 + depth).start()
 
     for early in (True, False):
 
@@ -143,7 +165,7 @@
         out_ref[:, :16, :] = main_s[: 4 * rows, :].reshape(dests, 16, LANES).astype(BF16)
 
 
-def fourier_blocks(control, spread, vertical, legendre, pair_base, dests):
+def fourier_blocks(control, spread, vertical, legendre, base, dests):
     pairs, slots, _, modes = control.shape
     rows = legendre.shape[2]
     ctrl = jnp.transpose(control, (0, 2, 3, 1))
@@ -155,15 +177,17 @@
         in_specs=[
             pl.BlockSpec(memory_space=pltpu.SMEM),
             pl.BlockSpec((4, 1, modes, slots), lambda t: (jnp.minimum(t, steps - 1), 0, 0, 0)),
-            pl.BlockSpec((modes, slots - 1), lambda t: (0, 0)),
-            pl.BlockSpec((modes, modes), lambda t: (0, 0)),
-            pl.BlockSpec((4, slots, rows), lambda t: (jnp.clip(t - 1, 0, steps - 1), 0, 0)),
+            pl.BlockSpec((modes, 4, slots - 1), lambda t: (0, 0, 0)),
+            pl.BlockSpec((modes, 4, modes), lambda t: (0, 0, 0)),
+            pl.BlockSpec(memory_space=pl.ANY),
         ],
         out_specs=pl.BlockSpec((dests, 32, LANES), lambda t: (0, jnp.maximum(t - 2, 0), 0)),
         scratch_shapes=[
             pltpu.VMEM((rows * 8, LANES), F32),
             pltpu.VMEM((steps, LANES, rows), F32),
             pltpu.VMEM((4 * LANES, rows), F32),
+            pltpu.VMEM((3, 4, slots, rows), BF16),
+            pltpu.SemaphoreType.DMA((3,)),
             pltpu.VMEM((modes, 9 * LANES), F32),
             pltpu.VMEM((modes, 6 * LANES), F32),
             pltpu.VMEM((modes, 6 * LANES), F32),
@@ -172,7 +196,13 @@
             pltpu.VMEM((144, modes), BF16),
         ],
         name="fourier",
-    )(pair_base, ctrl, jnp.transpose(spread), vertical, legendre)
+    )(
+        base,
+        ctrl,
+        jnp.transpose(spread, (2, 0, 1)),
+        jnp.transpose(vertical, (1, 0, 2)),
+        legendre,
+    )
 
 
 def cosine(turns):
@@ -396,9 +426,10 @@
     device_count = wave_count * lax.axis_size("lat")
     cols = column_index.shape[0]
     slots = max(2, 2 * cols // device_count)
-    var = lax.axis_index("lat") // 2
-    pair_base = (lax.axis_index("wave") * pairs).astype(jnp.int32).reshape(1)
-    blocks = fourier_blocks(control, spread[var], vertical[var], legendre, pair_base, device_count)
+    base = jnp.stack([lax.axis_index("wave") * pairs, lax.axis_index("lat") // 2])
+    blocks = fourier_blocks(
+        control, spread, vertical, legendre, base.astype(jnp.int32), device_count
+    )
     index = column_index.reshape(1, cols)
     main_table, row, spot = tables(
         index, column_owner.reshape(1, cols), 4 * pairs * wave_count, slots

time: 178 us -> 175 us (0.983)
  local copies, waits for them, and re-layouts: 4.16 us -> 0.03 us
    unnamed x12 -> x8, local copies, waits for them, and re-layouts: 2.76 us -> 0.03 us
where the time goes in v6:
time: 175 us; the launch traced here: 174 us
  waiting for transfers between devices  66.9 us (38%)
  blocking collectives  63.9 us (37%)
  Pallas kernels  30.4 us (17%)
  starting transfers between devices  11.9 us (7%)
    all_to_all x1, waiting for transfers between devices, exchange(): lax.all_to_all(x, ('wave', 'lat'), split_axis=0, concat_axis=0, tiled=True)  66.9 us
    all_to_all x2, blocking collectives, exchange(): lax.all_to_all(x, ('wave', 'lat'), split_axis=0, concat_axis=0, tiled=True)  63.9 us
    pallas_call x1, Pallas kernels, fourier_blocks(): pl.pallas_call(fourier_kernel, out_shape=jax.ShapeDtypeStruct((dests, 32...  15 us
    all_to_all x1, starting transfers between devices, exchange(): lax.all_to_all(x, ('wave', 'lat'), split_axis=0, concat_axis=0, tiled=True)  11.9 us
    pallas_call x1, Pallas kernels, column_states(): pl.pallas_call(state_kernel, out_shape=jax.ShapeDtypeStruct((total, 5 * L...  7.63 us
  transfers between devices with their start and end apart: 1, of which 1 were waited for; matrix products, arithmetic and copies ran while one was open for 0% of the time, Pallas kernels for 2%

profile of v6, /device:TPU:1, one launch (start us, length us, event | category | flops | bytes accessed | tf_op | source)
XLA Modules:
  0.0 174.5 jit_solution(7155473366381055894)
XLA Ops:
  0.6 0.7 pad_add_fusion.base_ref
  1.3 15.0 %fourier.1 = bf16[128,176,128]{2,1,0:T(8,128)(2,1)} custom-call(s32[2]{0:T(128)} %pad_add_fusion.base_ref, bf16[20,1,137,641]{3,2,1,0:T(8,128)(2,1)} %bitcast.24, f32[137,4,640]{2,1,0:T(4,128)} %bitcast.25, bf16[137,4,137]{2,1,0:T(4,128)(2,1)} %bitcast.26, bf16[20,641,512]{2,1,0:T(8,128)(2,1)} %leg_ref.1), custom_call_target="tpu_custom_call" | custom-call | tf_op jit(solution)/shard_map/fourier/pallas_call | solution.py:173
  16.3 0.0 copy-start.2
  16.3 0.0 copy-start.3
  16.3 11.9 %all-to-all-start = ((bf16[128,176,128]{2,1,0:T(8,128)(2,1)}), bf16[128,176,128]{2,1,0:T(8,128)(2,1)}, u32[]{:S(2)}, u32[]{:S(2)}) async-start(bf16[128,176,128]{2,1,0:T(8,128)(2,1)} %fourier.1), calls=%async_computation | async-start | bytes 11534336 | tf_op jit(solution)/shard_map/all_to_all | solution.py:420
  28.2 0.0 copy-done.2
  28.2 0.0 copy-done.3
  28.2 2.7 %tables.1 = (bf16[512,1280]{1,0:T(8,128)(2,1)S(1)}, f32[512,128]{1,0:T(8,128)S(1)}, s32[1,512]{1,0:T(1,128)S(1)}) custom-call(s32[1,512]{1,0:T(1,128)S(1)} %bitcast.22, s32[1,512]{1,0:T(1,128)S(1)} %bitcast.23), custom_call_target="tpu_custom_call" | custom-call | flops 39321600 | bytes 4194304 | tf_op jit(solution)/shard_map/tables/pallas_call | solution.py:257
  30.9 66.9 %all-to-all-done = bf16[128,176,128]{2,1,0:T(8,128)(2,1)} async-done(((bf16[128,176,128]{2,1,0:T(8,128)(2,1)}), bf16[128,176,128]{2,1,0:T(8,128)(2,1)}, u32[]{:S(2)}, u32[]{:S(2)}) %all-to-all-start) | async-done | bytes 5767200 | tf_op jit(solution)/shard_map/all_to_all | solution.py:420
  97.8 7.6 %states.1 = bf16[1024,640]{1,0:T(8,128)(2,1)S(1)} custom-call(bf16[512,1280]{1,0:T(8,128)(2,1)S(1)} %get-tuple-element.8.main_ref, s32[1,512]{1,0:T(1,128)S(1)} %get-tuple-element.7.spot_ref, f32[512,128]{1,0:T(8,128)S(1)} %get-tuple-element.9.row_ref, bf16[16,1408,128]{2,1,0:T(8,128)(2,1)} %bitcast.7.coeff_ref), custom_call_target="tpu_custom_call" | custom-call | tf_op jit(solution)/shard_map/states/pallas_call | solution.py:324
  105.4 0.0 copy-start
  105.4 0.0 copy-start.1
  105.4 29.2 %all_to_all.15 = bf16[128,8,640]{2,1,0:T(8,128)(2,1)S(1)} all-to-all(bf16[128,8,640]{2,1,0:T(8,128)(2,1)S(1)} %bitcast.19), channel_id=1, replica_groups=mesh['wave'=16,'lat'=8] {'wave','lat'}, dimensions={0} | all-to-all | bytes 2621440 | tf_op jit(solution)/shard_map/all_to_all | solution.py:420
  134.6 0.0 copy-done
  134.6 0.0 copy-done.1
  134.6 2.6 %answers.1 = bf16[1024,1024]{1,0:T(8,128)(2,1)S(1)} custom-call(bf16[1024,640]{1,0:T(8,128)(2,1)S(1)} %bitcast.20, bf16[548,366]{1,0:T(8,128)(2,1)S(1)} %bitcast.21, f32[1,366]{1,0:T(1,128)S(1)} %copy-done.1), custom_call_target="tpu_custom_call" | custom-call | tf_op jit(solution)/shard_map/answers/pallas_call | solution.py:377
  137.2 34.7 %all_to_all.16 = bf16[128,8,1024]{2,1,0:T(8,128)(2,1)S(1)} all-to-all(bf16[128,8,1024]{2,1,0:T(8,128)(2,1)S(1)} %bitcast.17), channel_id=1, replica_groups=mesh['wave'=16,'lat'=8] {'wave','lat'}, dimensions={0} | all-to-all | bytes 4194304 | tf_op jit(solution)/shard_map/all_to_all | solution.py:420
  171.9 2.5 %collect.1 = (bf16[366,512]{1,0:T(8,128)(2,1)}, bf16[548,512]{1,0:T(8,128)(2,1)}) custom-call(s32[1,512]{1,0:T(1,128)S(1)} %get-tuple-element.7.spot_ref, bf16[1024,1024]{1,0:T(8,128)(2,1)S(1)} %bitcast.18), custom_call_target="tpu_custom_call" | custom-call | tf_op jit(solution)/shard_map/collect/pallas_call | solution.py:408
Async XLA Ops:
  16.3 11.9 %copy-start.2 = (s32[512]{0:T(512)S(1)}, s32[512]{0:T(512)}, u32[]{:S(2)}) copy-start(s32[512]{0:T(512)} %param.12) | copy-start | bytes 6148
  16.3 11.9 %copy-start.3 = (s32[512,1]{0,1:T(1,128)S(1)}, s32[512,1]{0,1:T(1,128)}, u32[]{:S(2)}) copy-start(s32[512,1]{0,1:T(1,128)} %param.13) | copy-start | bytes 6148
  16.3 81.5 %all-to-all-start = ((bf16[128,176,128]{2,1,0:T(8,128)(2,1)}), bf16[128,176,128]{2,1,0:T(8,128)(2,1)}, u32[]{:S(2)}, u32[]{:S(2)}) async-start(bf16[128,176,128]{2,1,0:T(8,128)(2,1)} %fourier.1), calls=%async_computation | async-start | bytes 11534336 | tf_op jit(solution)/shard_map/all_to_all | solution.py:420
  105.4 29.2 %copy-start = (bf16[1,366,548]{1,2,0:T(8,128)(2,1)S(1)}, bf16[1,366,548]{1,2,0:T(8,128)(2,1)}, u32[]{:S(2)}) copy-start(bf16[1,366,548]{1,2,0:T(8,128)(2,1)} %param.14) | copy-start | bytes 1203412
  105.4 29.2 %copy-start.1 = (f32[1,366]{1,0:T(1,128)S(1)}, f32[1,366]{1,0:T(1,128)}, u32[]{:S(2)}) copy-start(f32[1,366]{1,0:T(1,128)} %bias_ref.1) | copy-start | bytes 4396

commit v7 on v6

--- a/solution.py
+++ b/solution.py
@@ -23,6 +23,7 @@
 
 def fourier_kernel(
     base_ref,
+    var_ref,
     ctrl_ref,
     spread_ref,
     vert_ref,
@@ -39,6 +40,7 @@
     scaled_s,
     spec_s,
     vert_s,
+    wide_s,
 ):
     slots = ctrl_ref.shape[3]
     waves = slots - 1
@@ -118,13 +120,13 @@
     def _():
         for step in range(depth):
             fetch(step).start()
-        mine = lax.broadcasted_iota(jnp.int32, (1, 4, 1), 1) == base_ref[1]
-        spread = jnp.sum(jnp.where(mine, spread_ref[...], 0.0), axis=1)
+        spread = spread_ref[:, var_ref[0], :]
         spread_s[:, waves:] = jnp.zeros((modes, spread_s.shape[1] - waves), F32)
         spread_s[:, :waves] = spread
         second_s[:, :waves] = pltpu.roll(spread, 1, 1)
         second_s[:, waves : waves + 1] = spread[:, waves - 1 :]
-        vert = jnp.sum(jnp.where(mine, vert_ref[...].astype(F32), 0.0), axis=1)
+        wide_s[...] = vert_ref[...].astype(F32)
+        vert = wide_s[:, var_ref[0], :]
         vert_s[...] = jnp.zeros_like(vert_s)
         vert_s[:modes, :] = vert.astype(BF16)
         rem_s[...] = jnp.zeros_like(rem_s)
@@ -165,7 +167,7 @@
         out_ref[:, :16, :] = main_s[: 4 * rows, :].reshape(dests, 16, LANES).astype(BF16)
 
 
-def fourier_blocks(control, spread, vertical, legendre, base, dests):
+def fourier_blocks(control, spread, vertical, legendre, base, var, dests):
     pairs, slots, _, modes = control.shape
     rows = legendre.shape[2]
     ctrl = jnp.transpose(control, (0, 2, 3, 1))
@@ -175,6 +177,7 @@
         out_shape=jax.ShapeDtypeStruct((dests, 32 * steps + 16, LANES), BF16),
         grid=(steps + 3,),
         in_specs=[
+            pl.BlockSpec(memory_space=pltpu.SMEM),
             pl.BlockSpec(memory_space=pltpu.SMEM),
             pl.BlockSpec((4, 1, modes, slots), lambda t: (jnp.minimum(t, steps - 1), 0, 0, 0)),
             pl.BlockSpec((modes, 4, slots - 1), lambda t: (0, 0, 0)),
@@ -194,10 +197,12 @@
             pltpu.VMEM((modes, 6 * LANES), BF16),
             pltpu.VMEM((4, 144, slots), BF16),
             pltpu.VMEM((144, modes), BF16),
+            pltpu.VMEM((modes, 4, modes), F32),
         ],
         name="fourier",
     )(
         base,
+        var,
         ctrl,
         jnp.transpose(spread, (2, 0, 1)),
         jnp.transpose(vertical, (1, 0, 2)),
@@ -426,10 +431,9 @@
     device_count = wave_count * lax.axis_size("lat")
     cols = column_index.shape[0]
     slots = max(2, 2 * cols // device_count)
-    base = jnp.stack([lax.axis_index("wave") * pairs, lax.axis_index("lat") // 2])
-    blocks = fourier_blocks(
-        control, spread, vertical, legendre, base.astype(jnp.int32), device_count
-    )
+    base = (lax.axis_index("wave") * pairs).astype(jnp.int32).reshape(1)
+    var = (lax.axis_index("lat") // 2).astype(jnp.int32).reshape(1)
+    blocks = fourier_blocks(control, spread, vertical, legendre, base, var, device_count)
     index = column_index.reshape(1, cols)
     main_table, row, spot = tables(
         index, column_owner.reshape(1, cols), 4 * pairs * wave_count, slots

time: 175 us -> 173 us (0.989)
  no operation moved by 1% of the time
where the time goes in v7:
time: 173 us
  waiting for transfers between devices  66.9 us (39%)
  blocking collectives  63.9 us (37%)
  Pallas kernels  29.4 us (17%)
  starting transfers between devices  11.9 us (7%)
    all_to_all x1, waiting for transfers between devices, exchange(): lax.all_to_all(x, ('wave', 'lat'), split_axis=0, concat_axis=0, tiled=True)  66.9 us
    all_to_all x2, blocking collectives, exchange(): lax.all_to_all(x, ('wave', 'lat'), split_axis=0, concat_axis=0, tiled=True)  63.9 us
    pallas_call x1, Pallas kernels, fourier_blocks(): pl.pallas_call(fourier_kernel, out_shape=jax.ShapeDtypeStruct((dests, 32...  14 us
    all_to_all x1, starting transfers between devices, exchange(): lax.all_to_all(x, ('wave', 'lat'), split_axis=0, concat_axis=0, tiled=True)  11.9 us
    pallas_call x1, Pallas kernels, column_states(): pl.pallas_call(state_kernel, out_shape=jax.ShapeDtypeStruct((total, 5 * L...  7.63 us
  transfers between devices with their start and end apart: 1, of which 1 were waited for; matrix products, arithmetic and copies ran while one was open for 0% of the time, Pallas kernels for 2%

profile of v7, /device:TPU:1, one launch (start us, length us, event | category | flops | bytes accessed | tf_op | source)
XLA Modules:
  0.0 172.8 jit_solution(7104321196933334192)
XLA Ops:
  0.6 14.0 %fourier.1 = bf16[128,176,128]{2,1,0:T(8,128)(2,1)} custom-call(s32[1]{0:T(128)} %bitcast.2.base_ref, s32[1]{0:T(128)} %bitcast.3.var_ref, bf16[20,1,137,641]{3,2,1,0:T(8,128)(2,1)} %bitcast.24, f32[137,4,640]{2,1,0:T(4,128)} %bitcast.25, bf16[137,4,137]{2,1,0:T(4,128)(2,1)} %bitcast.26, bf16[20,641,512]{2,1,0:T(8,128)(2,1)} %leg_ref.1), custom_call_target="tpu_custom_call" | custom-call | tf_op jit(solution)/shard_map/fourier/pallas_call | solution.py:175
  14.7 0.0 copy-start.2
  14.7 0.0 copy-start.3
  14.7 11.9 %all-to-all-start = ((bf16[128,176,128]{2,1,0:T(8,128)(2,1)}), bf16[128,176,128]{2,1,0:T(8,128)(2,1)}, u32[]{:S(2)}, u32[]{:S(2)}) async-start(bf16[128,176,128]{2,1,0:T(8,128)(2,1)} %fourier.1), calls=%async_computation | async-start | bytes 11534336 | tf_op jit(solution)/shard_map/all_to_all | solution.py:425
  26.5 0.0 copy-done.2
  26.5 0.0 copy-done.3
  26.6 2.7 %tables.1 = (bf16[512,1280]{1,0:T(8,128)(2,1)S(1)}, f32[512,128]{1,0:T(8,128)S(1)}, s32[1,512]{1,0:T(1,128)S(1)}) custom-call(s32[1,512]{1,0:T(1,128)S(1)} %bitcast.22, s32[1,512]{1,0:T(1,128)S(1)} %bitcast.23), custom_call_target="tpu_custom_call" | custom-call | flops 39321600 | bytes 4194304 | tf_op jit(solution)/shard_map/tables/pallas_call | solution.py:262
  29.3 66.9 %all-to-all-done = bf16[128,176,128]{2,1,0:T(8,128)(2,1)} async-done(((bf16[128,176,128]{2,1,0:T(8,128)(2,1)}), bf16[128,176,128]{2,1,0:T(8,128)(2,1)}, u32[]{:S(2)}, u32[]{:S(2)}) %all-to-all-start) | async-done | bytes 5767200 | tf_op jit(solution)/shard_map/all_to_all | solution.py:425
  96.1 7.6 %states.1 = bf16[1024,640]{1,0:T(8,128)(2,1)S(1)} custom-call(bf16[512,1280]{1,0:T(8,128)(2,1)S(1)} %get-tuple-element.8.main_ref, s32[1,512]{1,0:T(1,128)S(1)} %get-tuple-element.7.spot_ref, f32[512,128]{1,0:T(8,128)S(1)} %get-tuple-element.9.row_ref, bf16[16,1408,128]{2,1,0:T(8,128)(2,1)} %bitcast.7.coeff_ref), custom_call_target="tpu_custom_call" | custom-call | tf_op jit(solution)/shard_map/states/pallas_call | solution.py:329
  103.7 0.0 copy-start
  103.8 0.0 copy-start.1
  103.8 29.2 %all_to_all.15 = bf16[128,8,640]{2,1,0:T(8,128)(2,1)S(1)} all-to-all(bf16[128,8,640]{2,1,0:T(8,128)(2,1)S(1)} %bitcast.19), channel_id=1, replica_groups=mesh['wave'=16,'lat'=8] {'wave','lat'}, dimensions={0} | all-to-all | bytes 2621440 | tf_op jit(solution)/shard_map/all_to_all | solution.py:425
  132.9 0.0 copy-done
  132.9 0.0 copy-done.1
  132.9 2.6 %answers.1 = bf16[1024,1024]{1,0:T(8,128)(2,1)S(1)} custom-call(bf16[1024,640]{1,0:T(8,128)(2,1)S(1)} %bitcast.20, bf16[548,366]{1,0:T(8,128)(2,1)S(1)} %bitcast.21, f32[1,366]{1,0:T(1,128)S(1)} %copy-done.1), custom_call_target="tpu_custom_call" | custom-call | tf_op jit(solution)/shard_map/answers/pallas_call | solution.py:382
  135.5 34.7 %all_to_all.16 = bf16[128,8,1024]{2,1,0:T(8,128)(2,1)S(1)} all-to-all(bf16[128,8,1024]{2,1,0:T(8,128)(2,1)S(1)} %bitcast.17), channel_id=1, replica_groups=mesh['wave'=16,'lat'=8] {'wave','lat'}, dimensions={0} | all-to-all | bytes 4194304 | tf_op jit(solution)/shard_map/all_to_all | solution.py:425
  170.3 2.5 %collect.1 = (bf16[366,512]{1,0:T(8,128)(2,1)}, bf16[548,512]{1,0:T(8,128)(2,1)}) custom-call(s32[1,512]{1,0:T(1,128)S(1)} %get-tuple-element.7.spot_ref, bf16[1024,1024]{1,0:T(8,128)(2,1)S(1)} %bitcast.18), custom_call_target="tpu_custom_call" | custom-call | tf_op jit(solution)/shard_map/collect/pallas_call | solution.py:413
Async XLA Ops:
  14.7 11.9 %copy-start.2 = (s32[512]{0:T(512)S(1)}, s32[512]{0:T(512)}, u32[]{:S(2)}) copy-start(s32[512]{0:T(512)} %param.12) | copy-start | bytes 6148
  14.7 11.9 %copy-start.3 = (s32[512,1]{0,1:T(1,128)S(1)}, s32[512,1]{0,1:T(1,128)}, u32[]{:S(2)}) copy-start(s32[512,1]{0,1:T(1,128)} %param.13) | copy-start | bytes 6148
  14.7 81.4 %all-to-all-start = ((bf16[128,176,128]{2,1,0:T(8,128)(2,1)}), bf16[128,176,128]{2,1,0:T(8,128)(2,1)}, u32[]{:S(2)}, u32[]{:S(2)}) async-start(bf16[128,176,128]{2,1,0:T(8,128)(2,1)} %fourier.1), calls=%async_computation | async-start | bytes 11534336 | tf_op jit(solution)/shard_map/all_to_all | solution.py:425
  103.7 29.2 %copy-start = (bf16[1,366,548]{1,2,0:T(8,128)(2,1)S(1)}, bf16[1,366,548]{1,2,0:T(8,128)(2,1)}, u32[]{:S(2)}) copy-start(bf16[1,366,548]{1,2,0:T(8,128)(2,1)} %param.14) | copy-start | bytes 1203412
  103.8 29.2 %copy-start.1 = (f32[1,366]{1,0:T(1,128)S(1)}, f32[1,366]{1,0:T(1,128)}, u32[]{:S(2)}) copy-start(f32[1,366]{1,0:T(1,128)} %bias_ref.1) | copy-start | bytes 4396

commit v8 on v7

--- a/solution.py
+++ b/solution.py
@@ -325,18 +325,18 @@
     sources, rows, _ = coeff.shape
     cols, depth = main_table.shape
     total = slots * LANES
-    whole = lambda x: pl.BlockSpec(x.shape, lambda v: (0,) * x.ndim)
+    whole = pl.BlockSpec(memory_space=pltpu.VMEM)
     return pl.pallas_call(
         state_kernel,
         out_shape=jax.ShapeDtypeStruct((total, 5 * LANES), BF16),
         grid=(4,),
         in_specs=[
-            whole(main_table),
-            whole(spot),
-            whole(row),
+            whole,
+            whole,
+            whole,
             pl.BlockSpec((sources, rows // 4, LANES), lambda v: (0, v, 0)),
         ],
-        out_specs=pl.BlockSpec((total, 5 * LANES), lambda v: (0, 0)),
+        out_specs=whole,
         scratch_shapes=[
             pltpu.VMEM((depth, 4 * LANES), BF16),
             pltpu.VMEM((2 * depth, LANES), F32),
@@ -353,42 +353,35 @@
     levels = jac_ref.shape[0] // 4
     rest = levels - LANES
 
-    @pl.when(pl.program_id(0) == 0)
-    def _():
-        jac = jac_ref[...].astype(F32)
-        jac_s[...] = jnp.zeros_like(jac_s)
-        for v in range(4):
-            at = v * levels
-            jac_s[v * LANES : (v + 1) * LANES, :] = jac[at : at + LANES].astype(BF16)
-            lo = 4 * LANES + (v % 2 * 2 + v // 2) * SLOT_LANES
-            piece = jnp.concatenate(
-                [jac[at + LANES : at + levels], jnp.zeros((16 - rest, channels), F32)], axis=0
-            )
-            jac_s[lo : lo + 16, :] = piece.astype(BF16)
-
-    depart = dot(state_ref[...], jac_s[...]) + bias_ref[...]
-    weighted = (depart / jnp.sqrt(1.0 + depart * depart * 0.25)).astype(BF16)
-    out_ref[:, :channels] = depart.astype(BF16)
-    out_ref[:, 3 * LANES : 3 * LANES + jac_ref.shape[0]] = lax.dot_general(
-        weighted, jac_ref[...], (((1,), (1,)), ((), ())), preferred_element_type=F32
-    ).astype(BF16)
+    jac = jac_ref[...].astype(F32)
+    jac_s[...] = jnp.zeros_like(jac_s)
+    for v in range(4):
+        at = v * levels
+        jac_s[v * LANES : (v + 1) * LANES, :] = jac[at : at + LANES].astype(BF16)
+        lo = 4 * LANES + (v % 2 * 2 + v // 2) * SLOT_LANES
+        piece = jnp.concatenate(
+            [jac[at + LANES : at + levels], jnp.zeros((16 - rest, channels), F32)], axis=0
+        )
+        jac_s[lo : lo + 16, :] = piece.astype(BF16)
+
+    total = state_ref.shape[0]
+    for lo in range(0, total, total // 2):
+        rows = slice(lo, lo + total // 2)
+        depart = dot(state_ref[rows, :], jac_s[...]) + bias_ref[...]
+        weighted = (depart / jnp.sqrt(1.0 + depart * depart * 0.25)).astype(BF16)
+        out_ref[rows, :channels] = depart.astype(BF16)
+        out_ref[rows, 3 * LANES : 3 * LANES + jac_ref.shape[0]] = lax.dot_general(
+            weighted, jac_ref[...], (((1,), (1,)), ((), ())), preferred_element_type=F32
+        ).astype(BF16)
 
 
 def answers(states, jac_t, bias):
     total, lanes = states.shape
     width, channels = jac_t.shape
     out_lanes = -(-channels // LANES) * LANES + -(-width // LANES) * LANES
-    steps = 2
     return pl.pallas_call(
         answer_kernel,
         out_shape=jax.ShapeDtypeStruct((total, out_lanes), BF16),
-        grid=(steps,),
-        in_specs=[
-            pl.BlockSpec((total // steps, lanes), lambda g: (g, 0)),
-            pl.BlockSpec((width, channels), lambda g: (0, 0)),
-            pl.BlockSpec((1, channels), lambda g: (0, 0)),
-        ],
-        out_specs=pl.BlockSpec((total // steps, out_lanes), lambda g: (g, 0)),
         scratch_shapes=[pltpu.VMEM((lanes, channels), BF16)],
         compiler_params=pltpu.CompilerParams(vmem_limit_bytes=20 << 20),
         name="answers",

time: 173 us -> 173 us (level)
  no operation moved by 1% of the time
where the time goes in v8:
time: 173 us; the launch traced here: 172 us
  waiting for transfers between devices  66.9 us (39%)
  blocking collectives  63.9 us (37%)
  Pallas kernels  29.1 us (17%)
  starting transfers between devices  11.9 us (7%)
    all_to_all x1, waiting for transfers between devices, exchange(): lax.all_to_all(x, ('wave', 'lat'), split_axis=0, concat_axis=0, tiled=True)  66.9 us
    all_to_all x2, blocking collectives, exchange(): lax.all_to_all(x, ('wave', 'lat'), split_axis=0, concat_axis=0, tiled=True)  63.9 us
    pallas_call x1, Pallas kernels, fourier_blocks(): pl.pallas_call(fourier_kernel, out_shape=jax.ShapeDtypeStruct((dests, 32...  14 us
    all_to_all x1, starting transfers between devices, exchange(): lax.all_to_all(x, ('wave', 'lat'), split_axis=0, concat_axis=0, tiled=True)  11.9 us
    pallas_call x1, Pallas kernels, column_states(): pl.pallas_call(state_kernel, out_shape=jax.ShapeDtypeStruct((total, 5 * L...  7.63 us
  transfers between devices with their start and end apart: 1, of which 1 were waited for; matrix products, arithmetic and copies ran while one was open for 0% of the time, Pallas kernels for 2%

profile of v8, /device:TPU:1, one launch (start us, length us, event | category | flops | bytes accessed | tf_op | source)
XLA Modules:
  0.0 172.5 jit_solution(10303603665597211325)
XLA Ops:
  0.6 14.0 %fourier.1 = bf16[128,176,128]{2,1,0:T(8,128)(2,1)} custom-call(s32[1]{0:T(128)} %bitcast.2.base_ref, s32[1]{0:T(128)} %bitcast.3.var_ref, bf16[20,1,137,641]{3,2,1,0:T(8,128)(2,1)} %bitcast.24, f32[137,4,640]{2,1,0:T(4,128)} %bitcast.25, bf16[137,4,137]{2,1,0:T(4,128)(2,1)} %bitcast.26, bf16[20,641,512]{2,1,0:T(8,128)(2,1)} %leg_ref.1), custom_call_target="tpu_custom_call" | custom-call | tf_op jit(solution)/shard_map/fourier/pallas_call | solution.py:175
  14.7 0.0 copy-start.2
  14.7 0.0 copy-start.3
  14.7 11.9 %all-to-all-start = ((bf16[128,176,128]{2,1,0:T(8,128)(2,1)}), bf16[128,176,128]{2,1,0:T(8,128)(2,1)}, u32[]{:S(2)}, u32[]{:S(2)}) async-start(bf16[128,176,128]{2,1,0:T(8,128)(2,1)} %fourier.1), calls=%async_computation | async-start | bytes 11534336 | tf_op jit(solution)/shard_map/all_to_all | solution.py:418
  26.5 0.0 copy-done.2
  26.6 0.0 copy-done.3
  26.6 2.7 %tables.1 = (bf16[512,1280]{1,0:T(8,128)(2,1)S(1)}, f32[512,128]{1,0:T(8,128)S(1)}, s32[1,512]{1,0:T(1,128)S(1)}) custom-call(s32[1,512]{1,0:T(1,128)S(1)} %bitcast.22, s32[1,512]{1,0:T(1,128)S(1)} %bitcast.23), custom_call_target="tpu_custom_call" | custom-call | flops 39321600 | bytes 4194304 | tf_op jit(solution)/shard_map/tables/pallas_call | solution.py:262
  29.3 66.9 %all-to-all-done = bf16[128,176,128]{2,1,0:T(8,128)(2,1)} async-done(((bf16[128,176,128]{2,1,0:T(8,128)(2,1)}), bf16[128,176,128]{2,1,0:T(8,128)(2,1)}, u32[]{:S(2)}, u32[]{:S(2)}) %all-to-all-start) | async-done | bytes 5767200 | tf_op jit(solution)/shard_map/all_to_all | solution.py:418
  96.1 7.6 %states.1 = bf16[1024,640]{1,0:T(8,128)(2,1)S(1)} custom-call(bf16[512,1280]{1,0:T(8,128)(2,1)S(1)} %get-tuple-element.8.main_ref, s32[1,512]{1,0:T(1,128)S(1)} %get-tuple-element.7.spot_ref, f32[512,128]{1,0:T(8,128)S(1)} %get-tuple-element.9.row_ref, bf16[16,1408,128]{2,1,0:T(8,128)(2,1)} %bitcast.7.coeff_ref), custom_call_target="tpu_custom_call" | custom-call | tf_op jit(solution)/shard_map/states/pallas_call | solution.py:329
  103.8 0.0 copy-start
  103.8 0.0 copy-start.1
  103.8 29.2 %all_to_all.15 = bf16[128,8,640]{2,1,0:T(8,128)(2,1)S(1)} all-to-all(bf16[128,8,640]{2,1,0:T(8,128)(2,1)S(1)} %bitcast.19), channel_id=1, replica_groups=mesh['wave'=16,'lat'=8] {'wave','lat'}, dimensions={0} | all-to-all | bytes 2621440 | tf_op jit(solution)/shard_map/all_to_all | solution.py:418
  132.9 0.0 copy-done
  132.9 0.0 copy-done.1
  132.9 2.3 %answers.1 = bf16[1024,1024]{1,0:T(8,128)(2,1)S(1)} custom-call(bf16[1024,640]{1,0:T(8,128)(2,1)S(1)} %bitcast.20, bf16[548,366]{1,0:T(8,128)(2,1)S(1)} %bitcast.21, f32[1,366]{1,0:T(1,128)S(1)} %copy-done.1), custom_call_target="tpu_custom_call" | custom-call | tf_op jit(solution)/shard_map/answers/pallas_call | solution.py:382
  135.2 34.7 %all_to_all.16 = bf16[128,8,1024]{2,1,0:T(8,128)(2,1)S(1)} all-to-all(bf16[128,8,1024]{2,1,0:T(8,128)(2,1)S(1)} %bitcast.17), channel_id=1, replica_groups=mesh['wave'=16,'lat'=8] {'wave','lat'}, dimensions={0} | all-to-all | bytes 4194304 | tf_op jit(solution)/shard_map/all_to_all | solution.py:418
  170.0 2.5 %collect.1 = (bf16[366,512]{1,0:T(8,128)(2,1)}, bf16[548,512]{1,0:T(8,128)(2,1)}) custom-call(s32[1,512]{1,0:T(1,128)S(1)} %get-tuple-element.7.spot_ref, bf16[1024,1024]{1,0:T(8,128)(2,1)S(1)} %bitcast.18), custom_call_target="tpu_custom_call" | custom-call | tf_op jit(solution)/shard_map/collect/pallas_call | solution.py:406
Async XLA Ops:
  14.7 11.9 %copy-start.2 = (s32[512]{0:T(512)S(1)}, s32[512]{0:T(512)}, u32[]{:S(2)}) copy-start(s32[512]{0:T(512)} %param.12) | copy-start | bytes 6148
  14.7 11.9 %copy-start.3 = (s32[512,1]{0,1:T(1,128)S(1)}, s32[512,1]{0,1:T(1,128)}, u32[]{:S(2)}) copy-start(s32[512,1]{0,1:T(1,128)} %param.13) | copy-start | bytes 6148
  14.7 81.4 %all-to-all-start = ((bf16[128,176,128]{2,1,0:T(8,128)(2,1)}), bf16[128,176,128]{2,1,0:T(8,128)(2,1)}, u32[]{:S(2)}, u32[]{:S(2)}) async-start(bf16[128,176,128]{2,1,0:T(8,128)(2,1)} %fourier.1), calls=%async_computation | async-start | bytes 11534336 | tf_op jit(solution)/shard_map/all_to_all | solution.py:418
  103.8 29.2 %copy-start = (bf16[1,366,548]{1,2,0:T(8,128)(2,1)S(1)}, bf16[1,366,548]{1,2,0:T(8,128)(2,1)}, u32[]{:S(2)}) copy-start(bf16[1,366,548]{1,2,0:T(8,128)(2,1)} %param.14) | copy-start | bytes 1203412
  103.8 29.2 %copy-start.1 = (f32[1,366]{1,0:T(1,128)S(1)}, f32[1,366]{1,0:T(1,128)}, u32[]{:S(2)}) copy-start(f32[1,366]{1,0:T(1,128)} %bias_ref.1) | copy-start | bytes 4396

commit v9 on v8

--- a/solution.py
+++ b/solution.py
@@ -189,8 +189,8 @@
             pltpu.VMEM((rows * 8, LANES), F32),
             pltpu.VMEM((steps, LANES, rows), F32),
             pltpu.VMEM((4 * LANES, rows), F32),
-            pltpu.VMEM((3, 4, slots, rows), BF16),
-            pltpu.SemaphoreType.DMA((3,)),
+            pltpu.VMEM((steps, 4, slots, rows), BF16),
+            pltpu.SemaphoreType.DMA((steps,)),
             pltpu.VMEM((modes, 9 * LANES), F32),
             pltpu.VMEM((modes, 6 * LANES), F32),
             pltpu.VMEM((modes, 6 * LANES), F32),

time: 173 us -> 174 us (level)
  no operation moved by 1% of the time
where the time goes in v9:
time: 174 us
  waiting for transfers between devices  66.9 us (38%)
  blocking collectives  63.9 us (37%)
  Pallas kernels  30.6 us (18%)
  starting transfers between devices  11.9 us (7%)
    all_to_all x1, waiting for transfers between devices, exchange(): lax.all_to_all(x, ('wave', 'lat'), split_axis=0, concat_axis=0, tiled=True)  66.9 us
    all_to_all x2, blocking collectives, exchange(): lax.all_to_all(x, ('wave', 'lat'), split_axis=0, concat_axis=0, tiled=True)  63.9 us
    pallas_call x1, Pallas kernels, fourier_blocks(): pl.pallas_call(fourier_kernel, out_shape=jax.ShapeDtypeStruct((dests, 32...  15.4 us
    all_to_all x1, starting transfers between devices, exchange(): lax.all_to_all(x, ('wave', 'lat'), split_axis=0, concat_axis=0, tiled=True)  11.9 us
    pallas_call x1, Pallas kernels, column_states(): pl.pallas_call(state_kernel, out_shape=jax.ShapeDtypeStruct((total, 5 * L...  7.63 us
  transfers between devices with their start and end apart: 1, of which 1 were waited for; matrix products, arithmetic and copies ran while one was open for 0% of the time, Pallas kernels for 2%

profile of v9, /device:TPU:1, one launch (start us, length us, event | category | flops | bytes accessed | tf_op | source)
XLA Modules:
  0.0 173.9 jit_solution(4704789255525512377)
XLA Ops:
  0.6 15.4 %fourier.1 = bf16[128,176,128]{2,1,0:T(8,128)(2,1)} custom-call(s32[1]{0:T(128)} %bitcast.2.base_ref, s32[1]{0:T(128)} %bitcast.3.var_ref, bf16[20,1,137,641]{3,2,1,0:T(8,128)(2,1)} %bitcast.24, f32[137,4,640]{2,1,0:T(4,128)} %bitcast.25, bf16[137,4,137]{2,1,0:T(4,128)(2,1)} %bitcast.26, bf16[20,641,512]{2,1,0:T(8,128)(2,1)} %leg_ref.1), custom_call_target="tpu_custom_call" | custom-call | tf_op jit(solution)/shard_map/fourier/pallas_call | solution.py:175
  16.1 0.0 copy-start.2
  16.1 0.0 copy-start.3
  16.1 11.9 %all-to-all-start = ((bf16[128,176,128]{2,1,0:T(8,128)(2,1)}), bf16[128,176,128]{2,1,0:T(8,128)(2,1)}, u32[]{:S(2)}, u32[]{:S(2)}) async-start(bf16[128,176,128]{2,1,0:T(8,128)(2,1)} %fourier.1), calls=%async_computation | async-start | bytes 11534336 | tf_op jit(solution)/shard_map/all_to_all | solution.py:418
  28.0 0.0 copy-done.2
  28.0 0.0 copy-done.3
  28.0 2.7 %tables.1 = (bf16[512,1280]{1,0:T(8,128)(2,1)S(1)}, f32[512,128]{1,0:T(8,128)S(1)}, s32[1,512]{1,0:T(1,128)S(1)}) custom-call(s32[1,512]{1,0:T(1,128)S(1)} %bitcast.22, s32[1,512]{1,0:T(1,128)S(1)} %bitcast.23), custom_call_target="tpu_custom_call" | custom-call | flops 39321600 | bytes 4194304 | tf_op jit(solution)/shard_map/tables/pallas_call | solution.py:262
  30.7 66.9 %all-to-all-done = bf16[128,176,128]{2,1,0:T(8,128)(2,1)} async-done(((bf16[128,176,128]{2,1,0:T(8,128)(2,1)}), bf16[128,176,128]{2,1,0:T(8,128)(2,1)}, u32[]{:S(2)}, u32[]{:S(2)}) %all-to-all-start) | async-done | bytes 5767200 | tf_op jit(solution)/shard_map/all_to_all | solution.py:418
  97.5 7.6 %states.1 = bf16[1024,640]{1,0:T(8,128)(2,1)S(1)} custom-call(bf16[512,1280]{1,0:T(8,128)(2,1)S(1)} %get-tuple-element.8.main_ref, s32[1,512]{1,0:T(1,128)S(1)} %get-tuple-element.7.spot_ref, f32[512,128]{1,0:T(8,128)S(1)} %get-tuple-element.9.row_ref, bf16[16,1408,128]{2,1,0:T(8,128)(2,1)} %bitcast.7.coeff_ref), custom_call_target="tpu_custom_call" | custom-call | tf_op jit(solution)/shard_map/states/pallas_call | solution.py:329
  105.2 0.0 copy-start
  105.2 0.0 copy-start.1
  105.2 29.2 %all_to_all.15 = bf16[128,8,640]{2,1,0:T(8,128)(2,1)S(1)} all-to-all(bf16[128,8,640]{2,1,0:T(8,128)(2,1)S(1)} %bitcast.19), channel_id=1, replica_groups=mesh['wave'=16,'lat'=8] {'wave','lat'}, dimensions={0} | all-to-all | bytes 2621440 | tf_op jit(solution)/shard_map/all_to_all | solution.py:418
  134.4 0.0 copy-done
  134.4 0.0 copy-done.1
  134.4 2.3 %answers.1 = bf16[1024,1024]{1,0:T(8,128)(2,1)S(1)} custom-call(bf16[1024,640]{1,0:T(8,128)(2,1)S(1)} %bitcast.20, bf16[548,366]{1,0:T(8,128)(2,1)S(1)} %bitcast.21, f32[1,366]{1,0:T(1,128)S(1)} %copy-done.1), custom_call_target="tpu_custom_call" | custom-call | tf_op jit(solution)/shard_map/answers/pallas_call | solution.py:382
  136.7 34.7 %all_to_all.16 = bf16[128,8,1024]{2,1,0:T(8,128)(2,1)S(1)} all-to-all(bf16[128,8,1024]{2,1,0:T(8,128)(2,1)S(1)} %bitcast.17), channel_id=1, replica_groups=mesh['wave'=16,'lat'=8] {'wave','lat'}, dimensions={0} | all-to-all | bytes 4194304 | tf_op jit(solution)/shard_map/all_to_all | solution.py:418
  171.4 2.5 %collect.1 = (bf16[366,512]{1,0:T(8,128)(2,1)}, bf16[548,512]{1,0:T(8,128)(2,1)}) custom-call(s32[1,512]{1,0:T(1,128)S(1)} %get-tuple-element.7.spot_ref, bf16[1024,1024]{1,0:T(8,128)(2,1)S(1)} %bitcast.18), custom_call_target="tpu_custom_call" | custom-call | tf_op jit(solution)/shard_map/collect/pallas_call | solution.py:406
Async XLA Ops:
  16.1 11.9 %copy-start.2 = (s32[512]{0:T(512)S(1)}, s32[512]{0:T(512)}, u32[]{:S(2)}) copy-start(s32[512]{0:T(512)} %param.12) | copy-start | bytes 6148
  16.1 11.9 %copy-start.3 = (s32[512,1]{0,1:T(1,128)S(1)}, s32[512,1]{0,1:T(1,128)}, u32[]{:S(2)}) copy-start(s32[512,1]{0,1:T(1,128)} %param.13) | copy-start | bytes 6148
  16.1 81.4 %all-to-all-start = ((bf16[128,176,128]{2,1,0:T(8,128)(2,1)}), bf16[128,176,128]{2,1,0:T(8,128)(2,1)}, u32[]{:S(2)}, u32[]{:S(2)}) async-start(bf16[128,176,128]{2,1,0:T(8,128)(2,1)} %fourier.1), calls=%async_computation | async-start | bytes 11534336 | tf_op jit(solution)/shard_map/all_to_all | solution.py:418
  105.2 29.2 %copy-start = (bf16[1,366,548]{1,2,0:T(8,128)(2,1)S(1)}, bf16[1,366,548]{1,2,0:T(8,128)(2,1)}, u32[]{:S(2)}) copy-start(bf16[1,366,548]{1,2,0:T(8,128)(2,1)} %param.14) | copy-start | bytes 1203412
  105.2 29.2 %copy-start.1 = (f32[1,366]{1,0:T(1,128)S(1)}, f32[1,366]{1,0:T(1,128)}, u32[]{:S(2)}) copy-start(f32[1,366]{1,0:T(1,128)} %bias_ref.1) | copy-start | bytes 4396
